TPU v7x, 128 devices: a whole 4x4x4 slice. The times are simulated.
128 devices in a mesh: wa: 4 (over z), facet: 32 (over x, y, core).
Axes of the slice: x: 4, y: 4, z: 4, core: 2. Of those that a mesh axis runs over, the one named last changes fastest.
Arguments:
- visibilities: bfloat16 [16384, 2, 64], P(('wa', 'facet')), may hold values from -6 to 6
- uv_angles: float32 [16384, 2, 64], P(('wa', 'facet')), may hold values from -3.140625 to 3.140625
- routes: int32 [16384, 1], P(('wa', 'facet')), may hold values from 0 to 127; in each aligned block of 128 rows (0 to 127, 128 to 255, ...) at most 2 rows name the same one
- offsets: int32 [16384, 2], P(('wa', 'facet')), may hold values from 0 to 448
- pixel_phase: float32 [32, 512, 512], P('facet'), may hold values from -3.140625 to 3.140625
Outputs:
- partial_images: float32 [4, 32, 512, 1024], P('wa', 'facet')
Inputs may be any that keep to these rules, and one draw needn't show every extreme that they name: `routes`: the subgrids of one device name each owner at most 2 times; some owner is named exactly 2 times.
All inputs are finite; a program needn't handle non-finite values.
Results may differ from a plain program's by a relative error of at most 0.0076.
Values may be sent and summed in bfloat16 or wider, within the bound.
A program may use at most 64 MiB of HBM per device.

v0:
```python
import math

import jax
import jax.numpy as jnp
from jax import lax
from jax.sharding import PartitionSpec as P

SUB = 64
GRID = 512


def from_behind(value, axis, by):
    devices = lax.axis_size(axis)
    pairs = [(i, i + by) for i in range(devices) if 0 <= i + by < devices]
    return lax.ppermute(value, axis, pairs)


def form_subgrids(vis_block, angle_block, sub_n):
    centred = (jnp.arange(sub_n) - sub_n // 2).astype(jnp.float32)
    count_vis = vis_block.shape[2]
    norm_scale = 1.0 / math.sqrt(count_vis)
    phase_u = centred[None, :, None] * angle_block[:, 0][:, None, :]
    phase_v = centred[None, :, None] * angle_block[:, 1][:, None, :]
    cos_u = jnp.cos(phase_u)
    sin_u = jnp.sin(phase_u)
    cos_v = jnp.cos(phase_v)
    sin_v = jnp.sin(phase_v)
    vis_re = vis_block[:, 0].astype(jnp.float32)[:, None, :]
    vis_im = vis_block[:, 1].astype(jnp.float32)[:, None, :]
    left_re = (cos_u * vis_re - sin_u * vis_im) * norm_scale
    left_im = (cos_u * vis_im + sin_u * vis_re) * norm_scale
    left_side = jnp.concatenate([left_re, left_im], axis=2).astype(jnp.bfloat16)
    right_side = jnp.concatenate(
        [jnp.concatenate([cos_v, -sin_v], axis=2), jnp.concatenate([sin_v, cos_v], axis=2)], axis=1
    ).astype(jnp.bfloat16)
    return jnp.einsum(
        "bak,bck->bac", left_side, right_side, preferred_element_type=jnp.float32
    ).astype(jnp.bfloat16)


def form_many(vis_all, angle_all, sub_n):
    total = vis_all.shape[0]
    count_vis = vis_all.shape[2]
    block_n = math.gcd(total, 8)
    vis_blocks = vis_all.reshape(total // block_n, block_n, 2, count_vis)
    angle_blocks = angle_all.reshape(total // block_n, block_n, 2, count_vis)
    formed = lax.map(
        lambda items: form_subgrids(items[0], items[1], sub_n), (vis_blocks, angle_blocks)
    )
    return formed.reshape(total, sub_n, 2 * sub_n)


def place_grid(sub_data, sub_offsets, sub_n, grid_n):
    slot_count = sub_data.shape[0]
    block_n = math.gcd(slot_count, 16)
    col_base = jnp.arange(2 * sub_n, dtype=jnp.int32)
    col_shift = col_base // sub_n * grid_n + col_base % sub_n
    targets = jnp.arange(2 * grid_n, dtype=jnp.int32)
    sub_line = jnp.arange(sub_n, dtype=jnp.int32)
    data_blocks = sub_data.reshape(slot_count // block_n, block_n, sub_n, 2 * sub_n)
    offset_blocks = sub_offsets.reshape(slot_count // block_n, block_n, 2)

    def add_piece(running_grid, items):
        piece_data, piece_offsets = items
        place_table = (
            col_shift[None, :, None] + piece_offsets[:, 1][:, None, None] == targets[None, None, :]
        ).astype(jnp.bfloat16)
        placed = jnp.einsum(
            "bcd,bdj->bcj", piece_data, place_table, preferred_element_type=jnp.float32
        )
        row_targets = (piece_offsets[:, 0][:, None] + sub_line[None, :]).reshape(-1)
        running_grid = running_grid.at[row_targets].add(placed.reshape(-1, 2 * grid_n))
        return (running_grid, None)

    start_grid = jnp.zeros((grid_n, 2 * grid_n), jnp.float32)
    final_grid, _ = lax.scan(add_piece, start_grid, (data_blocks, offset_blocks))
    return final_grid


def dft_tables(grid_n):
    index_line = jnp.arange(grid_n, dtype=jnp.int32)
    product = index_line[:, None] * index_line[None, :] % grid_n
    angle_table = product.astype(jnp.float32) * (2.0 * math.pi / grid_n)
    root_scale = 1.0 / math.sqrt(grid_n)
    cos_table = jnp.cos(angle_table) * root_scale
    sin_table = jnp.sin(angle_table) * root_scale
    row_table = jnp.concatenate([cos_table, sin_table], axis=0).astype(jnp.bfloat16)
    col_table = jnp.concatenate(
        [
            jnp.concatenate([cos_table, sin_table], axis=1),
            jnp.concatenate([-sin_table, cos_table], axis=1),
        ],
        axis=0,
    ).astype(jnp.bfloat16)
    return (row_table, col_table)


def inverse_dft(grid_bf, row_table, col_table, grid_n):
    stacked = jnp.dot(row_table, grid_bf, preferred_element_type=jnp.float32)
    half_re = stacked[:grid_n, :grid_n] - stacked[grid_n:, grid_n:]
    half_im = stacked[:grid_n, grid_n:] + stacked[grid_n:, :grid_n]
    half_band = jnp.concatenate([half_re, half_im], axis=1).astype(jnp.bfloat16)
    return jnp.dot(half_band, col_table, preferred_element_type=jnp.float32)


def phase_times(phase_re, phase_im, field, grid_n):
    field_re = field[..., :grid_n]
    field_im = field[..., grid_n:]
    return jnp.concatenate(
        [phase_re * field_re - phase_im * field_im, phase_re * field_im + phase_im * field_re],
        axis=-1,
    )


def on_device(visibilities, uv_angles, routes, offsets, pixel_phase):
    sub_count = visibilities.shape[0]
    wa_count = lax.axis_size("wa")
    facet_count = lax.axis_size("facet")
    owners_n = wa_count * facet_count
    capacity = max(2, (2 * sub_count + owners_n - 1) // owners_n)
    slots_n = owners_n * capacity
    owner_index = routes[:, 0]
    one_hot = (owner_index[:, None] == jnp.arange(owners_n, dtype=jnp.int32)[None, :]).astype(
        jnp.int32
    )
    slot_rank = jnp.sum(jnp.cumsum(one_hot, axis=0) * one_hot, axis=1) - 1
    slot_index = owner_index * capacity + slot_rank
    send_offsets = jnp.zeros((slots_n, 2), jnp.int32).at[slot_index].set(offsets)
    subgrids = form_many(visibilities, uv_angles, SUB)
    send_buffer = jnp.zeros((slots_n, SUB, 2 * SUB), jnp.bfloat16).at[slot_index].set(subgrids)
    flat_data = send_buffer.reshape(owners_n, capacity, SUB, 2 * SUB)
    flat_offsets = send_offsets.reshape(owners_n, capacity, 2)
    got_data, got_offsets = (
        lax.all_to_all(flat_data, ("wa", "facet"), split_axis=0, concat_axis=0, tiled=True),
        lax.all_to_all(flat_offsets, ("wa", "facet"), split_axis=0, concat_axis=0, tiled=True),
    )
    got_data = got_data.reshape(slots_n, SUB, 2 * SUB)
    got_offsets = got_offsets.reshape(slots_n, 2)
    facet_grid = place_grid(got_data, got_offsets, SUB, GRID).astype(jnp.bfloat16)
    row_table, col_table = dft_tables(GRID)
    image_band = inverse_dft(facet_grid, row_table, col_table, GRID)
    phase_re = jnp.cos(pixel_phase[0])
    phase_im = jnp.sin(pixel_phase[0])
    plane_index = lax.axis_index("wa")
    running = image_band
    for section in range(1, wa_count):
        incoming = from_behind(running, "wa", 1)
        candidate = phase_times(phase_re, phase_im, incoming, GRID) + image_band
        running = jnp.where(plane_index == section, candidate, running)
    return running.reshape(1, 1, GRID, 2 * GRID)


def solution(mesh):
    in_specs = (
        P(("wa", "facet"), None, None),
        P(("wa", "facet"), None, None),
        P(("wa", "facet"), None),
        P(("wa", "facet"), None),
        P("facet", None, None),
    )
    out_specs = P("wa", "facet", None, None)
    return jax.shard_map(
        on_device, mesh=mesh, in_specs=in_specs, out_specs=out_specs, check_vma=False
    )
```

profile of v0, /device:TPU:1, one launch (start us, length us, event | category | flops | bytes accessed | tf_op | source)
XLA Modules:
  0.0 557.1 jit_solution(4020004572472474905)
XLA Ops:
  5.6 11.5 %all-to-all-start = ((s32[128,2,2]{1,2,0:T(2,128)}), s32[128,2,2]{1,2,0:T(2,128)S(1)}, u32[]{:S(2)}, u32[]{:S(2)}) async-start(s32[128,2,2]{1,2,0:T(2,128)} %copy.14), calls=%async_computation | async-start | bytes 262144 | tf_op jit(solution)/shard_map/all_to_all | solution.py:135
  18.9 41.2 %while.23 = (s32[]{:T(128)}, bf16[16,8,64,128]{3,2,1,0:T(8,128)(2,1)S(1)}, f32[16,8,2,64]{3,1,0,2:T(8,128)S(1)}, bf16[16,8,2,64]{3,1,0,2:T(8,128)(2,1)S(1)}, s32[]{:T(128)}) while((s32[]{:T(128)}, bf16[16,8,64,128]{3,2,1,0:T(8,128)(2,1)S(1)}, f32[16,8,2,64]{3,1,0,2:T(8,128)S(1)}, bf16[16,8,2,64]{3,1,0,2:T(8,128)(2,1)S(1)}, s32[]{:T(128)}) %tuple.76), condition=%wide.region_3.4_spmd, body=%wide.region_2.3_spmd.sunk | while | flops 18678912 | bytes 1149513 | solution.py:47
  19.0 2.1 fusion.94
  21.6 2.1 fusion.94
  24.2 2.1 fusion.94
  26.7 2.1 fusion.94
  29.3 2.1 fusion.94
  31.9 2.1 fusion.94
  34.5 2.1 fusion.94
  37.0 2.1 fusion.94
  42.2 2.1 fusion.94
  47.3 2.1 fusion.94
  49.9 2.1 fusion.94
  55.1 2.1 fusion.94
  60.1 3.0 broadcast_in_dim.25
  63.2 15.7 %scatter_fusion.1 = bf16[256,64,128]{2,1,0:T(8,128)(2,1)} fusion(bf16[256,64,128]{2,1,0:T(8,128)(2,1)} %broadcast_in_dim.25, s32[128]{0:T(128)S(1)} %fusion.79, bf16[128,64,128]{2,1,0:T(8,128)(2,1)S(1)} %bitcast.115), kind=kCustom, calls=%fused_computation.2 | custom fusion | bytes 6291968 | tf_op jit(solution)/shard_map/scatter | solution.py:130
  78.9 10.2 %all-to-all-start.1 = ((bf16[128,2,64,128]{3,2,1,0:T(8,128)(2,1)}), bf16[128,2,64,128]{3,2,1,0:T(8,128)(2,1)}, u32[]{:S(2)}, u32[]{:S(2)}) async-start(bf16[128,2,64,128]{3,2,1,0:T(8,128)(2,1)} %bitcast.114), calls=%async_computation.1 | async-start | bytes 8388608 | tf_op jit(solution)/shard_map/all_to_all | solution.py:134
  89.1 4.7 negate_convert_fusion
  93.8 4.4 multiply_convert_fusion
  98.3 43.5 %all-to-all-done.1 = bf16[128,2,64,128]{3,2,1,0:T(8,128)(2,1)} async-done(((bf16[128,2,64,128]{3,2,1,0:T(8,128)(2,1)}), bf16[128,2,64,128]{3,2,1,0:T(8,128)(2,1)}, u32[]{:S(2)}, u32[]{:S(2)}) %all-to-all-start.1) | async-done | bytes 4194336 | tf_op jit(solution)/shard_map/all_to_all | solution.py:134
  142.1 257.4 %while.24 = (s32[]{:T(128)}, f32[512,1024]{1,0:T(8,128)S(1)}, s32[16,16,2]{1,0,2:T(8,128)S(1)}, bf16[16,16,64,128]{3,2,1,0:T(8,128)(2,1)}, s32[]{:T(128)}) while((s32[]{:T(128)}, f32[512,1024]{1,0:T(8,128)S(1)}, s32[16,16,2]{1,0,2:T(8,128)S(1)}, bf16[16,16,64,128]{3,2,1,0:T(8,128)(2,1)}, s32[]{:T(128)}) %tuple.72), condition=%wide.region_8.9_spmd.clone, body=%wide.region_6.8_spmd.clone.sunk | while | flops 271589120 | bytes 17082560 | solution.py:76
  142.2 4.7 fusion.98
  147.1 11.1 %scatter_fusion = f32[512,1024]{1,0:T(8,128)S(1)} fusion(f32[512,1024]{1,0:T(8,128)S(1)} %get-tuple-element.260, s32[1024]{0:T(1024)S(1)} %bitcast.117, f32[1024,1024]{1,0:T(8,128)} %bitcast.113), kind=kCustom, calls=%fused_computation.clone.clone.1 | custom fusion | flops 1048576 | bytes 12587008 | tf_op jit(solution)/shard_map/while/body/eval_jaxpr/scatter-add | solution.py:72
  158.3 4.7 fusion.98
  163.2 11.1 %scatter_fusion = f32[512,1024]{1,0:T(8,128)S(1)} fusion(f32[512,1024]{1,0:T(8,128)S(1)} %get-tuple-element.260, s32[1024]{0:T(1024)S(1)} %bitcast.117, f32[1024,1024]{1,0:T(8,128)} %bitcast.113), kind=kCustom, calls=%fused_computation.clone.clone.1 | custom fusion | flops 1048576 | bytes 12587008 | tf_op jit(solution)/shard_map/while/body/eval_jaxpr/scatter-add | solution.py:72
  174.4 4.7 fusion.98
  179.3 11.1 %scatter_fusion = f32[512,1024]{1,0:T(8,128)S(1)} fusion(f32[512,1024]{1,0:T(8,128)S(1)} %get-tuple-element.260, s32[1024]{0:T(1024)S(1)} %bitcast.117, f32[1024,1024]{1,0:T(8,128)} %bitcast.113), kind=kCustom, calls=%fused_computation.clone.clone.1 | custom fusion | flops 1048576 | bytes 12587008 | tf_op jit(solution)/shard_map/while/body/eval_jaxpr/scatter-add | solution.py:72
  190.5 4.7 fusion.98
  195.4 11.1 %scatter_fusion = f32[512,1024]{1,0:T(8,128)S(1)} fusion(f32[512,1024]{1,0:T(8,128)S(1)} %get-tuple-element.260, s32[1024]{0:T(1024)S(1)} %bitcast.117, f32[1024,1024]{1,0:T(8,128)} %bitcast.113), kind=kCustom, calls=%fused_computation.clone.clone.1 | custom fusion | flops 1048576 | bytes 12587008 | tf_op jit(solution)/shard_map/while/body/eval_jaxpr/scatter-add | solution.py:72
  206.6 4.7 fusion.98
  211.4 11.1 %scatter_fusion = f32[512,1024]{1,0:T(8,128)S(1)} fusion(f32[512,1024]{1,0:T(8,128)S(1)} %get-tuple-element.260, s32[1024]{0:T(1024)S(1)} %bitcast.117, f32[1024,1024]{1,0:T(8,128)} %bitcast.113), kind=kCustom, calls=%fused_computation.clone.clone.1 | custom fusion | flops 1048576 | bytes 12587008 | tf_op jit(solution)/shard_map/while/body/eval_jaxpr/scatter-add | solution.py:72
  222.7 4.7 fusion.98
  227.5 11.1 %scatter_fusion = f32[512,1024]{1,0:T(8,128)S(1)} fusion(f32[512,1024]{1,0:T(8,128)S(1)} %get-tuple-element.260, s32[1024]{0:T(1024)S(1)} %bitcast.117, f32[1024,1024]{1,0:T(8,128)} %bitcast.113), kind=kCustom, calls=%fused_computation.clone.clone.1 | custom fusion | flops 1048576 | bytes 12587008 | tf_op jit(solution)/shard_map/while/body/eval_jaxpr/scatter-add | solution.py:72
  238.8 4.7 fusion.98
  243.6 11.1 %scatter_fusion = f32[512,1024]{1,0:T(8,128)S(1)} fusion(f32[512,1024]{1,0:T(8,128)S(1)} %get-tuple-element.260, s32[1024]{0:T(1024)S(1)} %bitcast.117, f32[1024,1024]{1,0:T(8,128)} %bitcast.113), kind=kCustom, calls=%fused_computation.clone.clone.1 | custom fusion | flops 1048576 | bytes 12587008 | tf_op jit(solution)/shard_map/while/body/eval_jaxpr/scatter-add | solution.py:72
  254.8 4.7 fusion.98
  259.7 11.1 %scatter_fusion = f32[512,1024]{1,0:T(8,128)S(1)} fusion(f32[512,1024]{1,0:T(8,128)S(1)} %get-tuple-element.260, s32[1024]{0:T(1024)S(1)} %bitcast.117, f32[1024,1024]{1,0:T(8,128)} %bitcast.113), kind=kCustom, calls=%fused_computation.clone.clone.1 | custom fusion | flops 1048576 | bytes 12587008 | tf_op jit(solution)/shard_map/while/body/eval_jaxpr/scatter-add | solution.py:72
  270.9 4.7 fusion.98
  275.8 11.1 %scatter_fusion = f32[512,1024]{1,0:T(8,128)S(1)} fusion(f32[512,1024]{1,0:T(8,128)S(1)} %get-tuple-element.260, s32[1024]{0:T(1024)S(1)} %bitcast.117, f32[1024,1024]{1,0:T(8,128)} %bitcast.113), kind=kCustom, calls=%fused_computation.clone.clone.1 | custom fusion | flops 1048576 | bytes 12587008 | tf_op jit(solution)/shard_map/while/body/eval_jaxpr/scatter-add | solution.py:72
  287.0 4.7 fusion.98
  291.9 11.1 %scatter_fusion = f32[512,1024]{1,0:T(8,128)S(1)} fusion(f32[512,1024]{1,0:T(8,128)S(1)} %get-tuple-element.260, s32[1024]{0:T(1024)S(1)} %bitcast.117, f32[1024,1024]{1,0:T(8,128)} %bitcast.113), kind=kCustom, calls=%fused_computation.clone.clone.1 | custom fusion | flops 1048576 | bytes 12587008 | tf_op jit(solution)/shard_map/while/body/eval_jaxpr/scatter-add | solution.py:72
  303.1 4.7 fusion.98
  308.0 11.1 %scatter_fusion = f32[512,1024]{1,0:T(8,128)S(1)} fusion(f32[512,1024]{1,0:T(8,128)S(1)} %get-tuple-element.260, s32[1024]{0:T(1024)S(1)} %bitcast.117, f32[1024,1024]{1,0:T(8,128)} %bitcast.113), kind=kCustom, calls=%fused_computation.clone.clone.1 | custom fusion | flops 1048576 | bytes 12587008 | tf_op jit(solution)/shard_map/while/body/eval_jaxpr/scatter-add | solution.py:72
  319.2 4.7 fusion.98
  324.1 11.1 %scatter_fusion = f32[512,1024]{1,0:T(8,128)S(1)} fusion(f32[512,1024]{1,0:T(8,128)S(1)} %get-tuple-element.260, s32[1024]{0:T(1024)S(1)} %bitcast.117, f32[1024,1024]{1,0:T(8,128)} %bitcast.113), kind=kCustom, calls=%fused_computation.clone.clone.1 | custom fusion | flops 1048576 | bytes 12587008 | tf_op jit(solution)/shard_map/while/body/eval_jaxpr/scatter-add | solution.py:72
  335.3 4.7 fusion.98
  340.2 11.1 %scatter_fusion = f32[512,1024]{1,0:T(8,128)S(1)} fusion(f32[512,1024]{1,0:T(8,128)S(1)} %get-tuple-element.260, s32[1024]{0:T(1024)S(1)} %bitcast.117, f32[1024,1024]{1,0:T(8,128)} %bitcast.113), kind=kCustom, calls=%fused_computation.clone.clone.1 | custom fusion | flops 1048576 | bytes 12587008 | tf_op jit(solution)/shard_map/while/body/eval_jaxpr/scatter-add | solution.py:72
  351.4 4.7 fusion.98
  356.3 11.1 %scatter_fusion = f32[512,1024]{1,0:T(8,128)S(1)} fusion(f32[512,1024]{1,0:T(8,128)S(1)} %get-tuple-element.260, s32[1024]{0:T(1024)S(1)} %bitcast.117, f32[1024,1024]{1,0:T(8,128)} %bitcast.113), kind=kCustom, calls=%fused_computation.clone.clone.1 | custom fusion | flops 1048576 | bytes 12587008 | tf_op jit(solution)/shard_map/while/body/eval_jaxpr/scatter-add | solution.py:72
  367.5 4.7 fusion.98
  372.3 11.1 %scatter_fusion = f32[512,1024]{1,0:T(8,128)S(1)} fusion(f32[512,1024]{1,0:T(8,128)S(1)} %get-tuple-element.260, s32[1024]{0:T(1024)S(1)} %bitcast.117, f32[1024,1024]{1,0:T(8,128)} %bitcast.113), kind=kCustom, calls=%fused_computation.clone.clone.1 | custom fusion | flops 1048576 | bytes 12587008 | tf_op jit(solution)/shard_map/while/body/eval_jaxpr/scatter-add | solution.py:72
  383.6 4.7 fusion.98
  388.4 11.1 %scatter_fusion = f32[512,1024]{1,0:T(8,128)S(1)} fusion(f32[512,1024]{1,0:T(8,128)S(1)} %get-tuple-element.260, s32[1024]{0:T(1024)S(1)} %bitcast.117, f32[1024,1024]{1,0:T(8,128)} %bitcast.113), kind=kCustom, calls=%fused_computation.clone.clone.1 | custom fusion | flops 1048576 | bytes 12587008 | tf_op jit(solution)/shard_map/while/body/eval_jaxpr/scatter-add | solution.py:72
  403.2 2.7 collective-permute-start
  405.9 4.7 fusion.82
  410.5 37.2 %collective-permute-done = f32[512,1024]{1,0:T(8,128)} collective-permute-done((f32[512,1024]{1,0:T(8,128)S(1)}, f32[512,1024]{1,0:T(8,128)}, u32[]{:S(2)}, u32[]{:S(2)}) %collective-permute-start) | collective-permute-done | bytes 2097184 | tf_op jit(solution)/shard_map/ppermute | solution.py:15
  451.6 5.6 collective-permute-start.1
  457.1 41.4 %collective-permute-done.1 = f32[512,1024]{1,0:T(8,128)} collective-permute-done((f32[512,1024]{1,0:T(8,128)}, f32[512,1024]{1,0:T(8,128)}, u32[]{:S(2)}, u32[]{:S(2)}) %collective-permute-start.1) | collective-permute-done | bytes 2097184 | tf_op jit(solution)/shard_map/ppermute | solution.py:15
  498.5 2.4 fusion.67
  500.9 3.6 fusion.50
  504.5 5.7 %collective-permute-start.2 = (f32[512,1024]{1,0:T(8,128)}, f32[512,1024]{1,0:T(8,128)}, u32[]{:S(2)}, u32[]{:S(2)}) collective-permute-start(f32[512,1024]{1,0:T(8,128)} %fusion.50), channel_id=1, source_target_pairs={{0,32},{32,64},{64,96},{1,33},{33,65},{65,97},{2,34},{34,66},{66,9... | collective-permute-start | bytes 6291464 | tf_op jit(solution)/shard_map/ppermute | solution.py:15
  510.3 40.8 %collective-permute-done.2 = f32[512,1024]{1,0:T(8,128)} collective-permute-done((f32[512,1024]{1,0:T(8,128)}, f32[512,1024]{1,0:T(8,128)}, u32[]{:S(2)}, u32[]{:S(2)}) %collective-permute-start.2) | collective-permute-done | bytes 2097184 | tf_op jit(solution)/shard_map/ppermute | solution.py:15
  551.1 2.4 fusion.69
  553.5 3.6 fusion.52
  (235 shorter events, 33.7 us)
Async XLA Ops:
  5.6 73.3 %all-to-all-start = ((s32[128,2,2]{1,2,0:T(2,128)}), s32[128,2,2]{1,2,0:T(2,128)S(1)}, u32[]{:S(2)}, u32[]{:S(2)}) async-start(s32[128,2,2]{1,2,0:T(2,128)} %copy.14), calls=%async_computation | async-start | bytes 262144 | tf_op jit(solution)/shard_map/all_to_all | solution.py:135
  78.9 62.9 %all-to-all-start.1 = ((bf16[128,2,64,128]{3,2,1,0:T(8,128)(2,1)}), bf16[128,2,64,128]{3,2,1,0:T(8,128)(2,1)}, u32[]{:S(2)}, u32[]{:S(2)}) async-start(bf16[128,2,64,128]{3,2,1,0:T(8,128)(2,1)} %bitcast.114), calls=%async_computation.1 | async-start | bytes 8388608 | tf_op jit(solution)/shard_map/all_to_all | solution.py:134
  400.8 1.0 copy-start.1
  403.2 44.6 %collective-permute-start = (f32[512,1024]{1,0:T(8,128)S(1)}, f32[512,1024]{1,0:T(8,128)}, u32[]{:S(2)}, u32[]{:S(2)}) collective-permute-start(f32[512,1024]{1,0:T(8,128)S(1)} %fusion.42), channel_id=1, source_target_pairs={{0,32},{32,64},{64,96},{1,33},{33,65},{65,97},{2,34},{34,66},{66,9... | collective-permute-start | bytes 6291464 | tf_op jit(solution)/shard_map/ppermute | solution.py:15
  410.5 39.3 %copy-start = (f32[1,512,512]{2,1,0:T(8,128)}, f32[1,512,512]{2,1,0:T(8,128)S(1)}, u32[]{:S(2)}) copy-start(f32[1,512,512]{2,1,0:T(8,128)S(1)} %get-tuple-element.164) | copy-start | bytes 3145732
  451.6 46.9 %collective-permute-start.1 = (f32[512,1024]{1,0:T(8,128)}, f32[512,1024]{1,0:T(8,128)}, u32[]{:S(2)}, u32[]{:S(2)}) collective-permute-start(f32[512,1024]{1,0:T(8,128)} %add_select_fusion), channel_id=1, source_target_pairs={{0,32},{32,64},{64,96},{1,33},{33,65},{65,97},{2,34},{34,66},{66,9... | collective-permute-start | bytes 6291464 | tf_op jit(solution)/shard_map/ppermute | solution.py:15
  504.5 46.5 %collective-permute-start.2 = (f32[512,1024]{1,0:T(8,128)}, f32[512,1024]{1,0:T(8,128)}, u32[]{:S(2)}, u32[]{:S(2)}) collective-permute-start(f32[512,1024]{1,0:T(8,128)} %fusion.50), channel_id=1, source_target_pairs={{0,32},{32,64},{64,96},{1,33},{33,65},{65,97},{2,34},{34,66},{66,9... | collective-permute-start | bytes 6291464 | tf_op jit(solution)/shard_map/ppermute | solution.py:15
where the time goes:
time: 563 us; the launch traced here: 557 us
  other arithmetic  242 us (43%)
  waiting for transfers between devices  163 us (29%)
  matrix products  83.3 us (15%)
  starting transfers between devices  35.7 us (6%)
  local copies, waits for them, and re-layouts  31.3 us (6%)
    scatter-add x16, other arithmetic, add_piece(): running_grid.at[row_targets].add(placed.reshape(-1, 2 * grid_n))  177 us
    ppermute x3, waiting for transfers between devices, from_behind(): return lax.ppermute(value, axis, pairs)  119 us
    dot_general x16, matrix products, add_piece(): jnp.einsum('bcd,bdj->bcj', piece_data, place_table, preferred_element_typ...  75.3 us
    another operation x19, other arithmetic  43.5 us
    all_to_all x1, waiting for transfers between devices, on_device(): lax.all_to_all(flat_data, ('wa', 'facet'), split_axis=0, concat_axis=0, t...  43.5 us
    scatter x1, local copies, waits for them, and re-layouts, on_device(): jnp.zeros((slots_n, SUB, 2 * SUB), jnp.bfloat16).at[slot_index]  15.7 us
    ppermute x3, starting transfers between devices, from_behind(): return lax.ppermute(value, axis, pairs)  14 us
    all_to_all x1, starting transfers between devices, on_device(): lax.all_to_all(flat_offsets, ('wa', 'facet'), split_axis=0, concat_axis=0...  11.5 us
  transfers between devices with their start and end apart: 5, of which 4 were waited for; matrix products, arithmetic and copies ran while one was open for 13% of the time, Pallas kernels for 0%

commit v1 on v0

v1 whole, which is shorter than its diff:
```python
import functools
import math

import jax
import jax.numpy as jnp
import ml_dtypes
import numpy as np
from jax import lax
from jax.experimental import pallas as pl
from jax.experimental.pallas import tpu as pltpu
from jax.sharding import PartitionSpec as P

SUB = 64
GRID = 512
NVIS = 64
SUBS = 128
CAP = 2
KINDS = 4
ROWS = CAP * KINDS
CHUNK = 64
CHUNKS = GRID // CHUNK
UNROLL = 8
BF16 = jnp.bfloat16
F32 = jnp.float32
MESH = pl.DeviceIdType.MESH
VMEM = pl.BlockSpec(memory_space=pltpu.VMEM)
NT = (((1,), (1,)), ((), ()))


def sincos(x):
    h = x * 0.5
    q = h * h
    s = h + h * q * (
        -1.6666666666666602e-1
        + q * (8.333333333320001e-3
        + q * (-1.9841269829589539e-4
        + q * (2.7557314297030280e-6
        + q * (-2.5050747762850355e-8
        + q * 1.5891812000000000e-10))))
    )
    c = 1.0 + q * (
        -0.5
        + q * (4.16666666666665929218e-2
        + q * (-1.38888888888730564116e-3
        + q * (2.48015872888517045348e-5
        + q * (-2.75573141792967388112e-7
        + q * 2.08757008419747316778e-9))))
    )
    return 1.0 - 2.0 * s * s, 2.0 * s * c


def pack_kernel(vis_ref, ang_ref, route_ref, off_ref, send_ref):
    owner = route_ref[...]
    facet = owner % 32
    plane = owner // 32
    odd = facet % 2
    seat_odd = jnp.where(plane < 2, plane + 6, 7 - plane)
    seat = jnp.where(odd == 1, seat_odd, plane)
    device = (seat // 2) * 32 + (facet - odd) + seat % 2
    owner_b = jnp.broadcast_to(owner.astype(F32), (SUBS, SUBS))
    row_i = lax.broadcasted_iota(jnp.int32, (SUBS, SUBS), 0)
    col_i = lax.broadcasted_iota(jnp.int32, (SUBS, SUBS), 1)
    earlier = jnp.where((owner_b == owner_b.T) & (row_i < col_i), 1.0, 0.0)
    rank = jnp.sum(earlier, axis=0, keepdims=True).astype(jnp.int32)
    slot = device * CAP + rank
    total = SUBS * CAP
    col_key = jnp.concatenate([slot + kind * total for kind in range(KINDS)], axis=1)

    angle = ang_ref[...]
    high = angle.astype(BF16)
    low = (angle - high.astype(F32)).astype(BF16)
    off_u, off_v = off_ref[0:1, :], off_ref[1:2, :]
    meta = jnp.where(row_i == 0, off_u // 16, 0)
    meta = jnp.where(row_i == 1, off_u % 16, meta)
    meta = jnp.where(row_i == 2, off_v // 16, meta)
    meta = jnp.where(row_i == 3, off_v % 16, meta)
    meta = meta.astype(F32).astype(BF16)
    data = jnp.concatenate([high, low, vis_ref[...], meta], axis=1)

    for block in range(ROWS):
        row = lax.broadcasted_iota(jnp.int32, (SUBS, KINDS * SUBS), 0) + block * SUBS
        place = row % ROWS
        row_key = (place // CAP) * total + (row // ROWS) * CAP + place % CAP
        one_hot = jnp.where(row_key == col_key, 1.0, 0.0).astype(BF16)
        picked = lax.dot_general(one_hot, data, NT, preferred_element_type=F32)
        send_ref[pl.ds(block * SUBS, SUBS), :] = picked.astype(BF16)


def pack(vis, ang, route, off):
    return pl.pallas_call(
        pack_kernel,
        out_shape=jax.ShapeDtypeStruct((SUBS * ROWS, 128), BF16),
        in_specs=[VMEM] * 4,
        out_specs=VMEM,
        name="pack",
    )(vis, ang, route, off)


def complex_mul(a, b):
    return a[0] * b[0] - a[1] * b[1], a[0] * b[1] + a[1] * b[0]


def grid_kernel(
    recv_ref, gj_ref, wide, pos_v, pos_s, pos_sem, au_r, au_i, av_r, av_i, bu, bv, acc
):
    slots = SUBS * CAP
    wide[...] = recv_ref[...].astype(F32)

    lane8 = lax.broadcasted_iota(jnp.int32, (8, 128), 1)
    weight = jnp.where(lane8 == 0, 8192.0, 0.0)
    weight = jnp.where(lane8 == 1, 512.0, weight)
    weight = jnp.where(lane8 == 2, 16.0, weight)
    weight = jnp.where(lane8 == 3, 1.0, weight).astype(BF16)
    for j in range(CAP):
        meta = wide[pl.ds((KINDS - 1) * CAP + j, SUBS, stride=ROWS), :].astype(BF16)
        packed = lax.dot_general(weight, meta, NT, preferred_element_type=F32)
        pos_v[j] = packed.astype(jnp.int32)
    to_scalar = pltpu.make_async_copy(pos_v, pos_s, pos_sem)
    to_scalar.start()

    acc[...] = jnp.zeros_like(acc)

    group = 16
    first = lax.broadcasted_iota(jnp.int32, (group, 128), 1) < 64

    def tables(g, carry):
        for j in range(CAP):
            start = g * group

            def rows(kind):
                at = start * ROWS + kind * CAP + j
                return wide[pl.ds(at, group, stride=ROWS), :]

            cos_t, sin_t = sincos(rows(0) + rows(1))
            vis = rows(2) * (1.0 / math.sqrt(NVIS))
            cos_o, sin_o = pltpu.roll(cos_t, 64, 1), pltpu.roll(sin_t, 64, 1)
            vis_o = pltpu.roll(vis, 64, 1)
            vis2 = (vis, jnp.where(first, vis_o, -vis_o))
            slot = pl.multiple_of(start + j * SUBS, group)
            for side in range(2):
                if side == 0:
                    e1 = (jnp.where(first, cos_t, cos_o), jnp.where(first, sin_t, sin_o))
                else:
                    e1 = (jnp.where(first, cos_o, cos_t), jnp.where(first, sin_o, sin_t))
                e2 = complex_mul(e1, e1)
                e3 = complex_mul(e2, e1)
                e4 = complex_mul(e2, e2)
                e5 = complex_mul(e4, e1)
                e6 = complex_mul(e4, e2)
                e7 = complex_mul(e4, e3)
                e8 = complex_mul(e4, e4)
                e16 = complex_mul(e8, e8)
                e24 = complex_mul(e16, e8)
                e32 = complex_mul(e16, e16)
                one = (jnp.ones_like(cos_t), jnp.zeros_like(cos_t))
                for a, e in enumerate((one, e1, e2, e3, e4, e5, e6, e7)):
                    where = pl.ds(slot * 8 + a, group, stride=8)
                    if side == 0:
                        re, im = complex_mul(e, vis2)
                        au_r[where, :] = re
                        au_i[where, :] = im
                    else:
                        av_r[where, :] = jnp.where(first, e[0], -e[1])
                        av_i[where, :] = jnp.where(first, e[1], e[0])
                steps = bu if side == 0 else bv
                for b, e in enumerate((e8, e16, e24, e32)):
                    steps[2 * b, pl.ds(slot, group), :] = e[0]
                    steps[2 * b + 1, pl.ds(slot, group), :] = e[1]
        return carry

    lax.fori_loop(0, SUBS // group, tables, 0)
    to_scalar.wait()

    lane_in = lax.broadcasted_iota(jnp.int32, (SUB, 128), 1) % 64

    def form(slot):
        base = pl.multiple_of(slot * 8, 8)
        ur, ui = au_r[pl.ds(base, 8), :], au_i[pl.ds(base, 8), :]
        vr, vi = av_r[pl.ds(base, 8), :], av_i[pl.ds(base, 8), :]

        def step(table, b):
            return table[2 * b, pl.ds(slot, 1), :], table[2 * b + 1, pl.ds(slot, 1), :]

        left = [None] * 8
        right_r = [None] * 8
        right_i = [None] * 8
        left[4], right_r[4], right_i[4] = ur, vr, vi
        for b in range(4):
            br, bi = step(bu, b)
            x, y = br * ur, bi * ui
            left[3 - b] = x + y
            if b < 3:
                left[5 + b] = x - y
            br, bi = step(bv, b)
            x, y, z, w = br * vr, bi * vi, br * vi, bi * vr
            right_r[3 - b] = x + y
            right_i[3 - b] = z - w
            if b < 3:
                right_r[5 + b] = x - y
                right_i[5 + b] = z + w
        left = jnp.concatenate(left, axis=0).astype(BF16)
        right = jnp.concatenate(right_r + right_i, axis=0).astype(BF16)
        return lax.dot_general(left, right, NT, preferred_element_type=F32)

    def place(slot, sub):
        packed = pos_s[slot // SUBS, 0, slot % SUBS]
        off_u, off_v = packed // 512, packed % 512
        tile, shift = off_v // 64, off_v % 64
        near = jnp.where(lane_in >= shift, pltpu.roll(sub, shift, 1), 0.0)
        far = jnp.where(lane_in < shift, pltpu.roll(sub, shift + 64, 1), 0.0)
        acc[tile, pl.ds(off_u, SUB), :] += near
        acc[tile + 1, pl.ds(off_u, SUB), :] += far

    def work(i, carry):
        subs = [form(i * UNROLL + n) for n in range(UNROLL)]
        for n in range(UNROLL):
            place(i * UNROLL + n, subs[n])
        return carry

    lax.fori_loop(0, slots // UNROLL, work, 0)

    sign = jnp.where(lax.broadcasted_iota(jnp.int32, (GRID, 128), 1) < 64, -1.0, 1.0)
    for tile in range(GRID // SUB):
        here = acc[tile]
        cols = pl.ds(tile * 128, 128)
        gj_ref[pl.ds(0, GRID), cols] = here.astype(BF16)
        gj_ref[pl.ds(GRID, GRID), cols] = (pltpu.roll(here, 64, 1) * sign).astype(BF16)


def grid_owner(recv):
    slots = SUBS * CAP
    return pl.pallas_call(
        grid_kernel,
        out_shape=jax.ShapeDtypeStruct((2 * GRID, 2 * GRID), BF16),
        in_specs=[VMEM],
        out_specs=VMEM,
        scratch_shapes=[
            pltpu.VMEM((SUBS * ROWS, 128), F32),
            pltpu.VMEM((CAP, 8, 128), jnp.int32),
            pltpu.SMEM((CAP, 8, 128), jnp.int32),
            pltpu.SemaphoreType.DMA,
        ]
        + [pltpu.VMEM((slots * 8, 128), F32)] * 4
        + [pltpu.VMEM((8, slots, 128), F32)] * 2
        + [pltpu.VMEM((GRID // SUB + 1, GRID, 128), F32)],
        name="grid",
    )(recv)


def chain_kernel(
    gj_ref, row_ref, phase_ref, out_ref, col, phase, from_h, from_s, mine,
    h_recv, s_recv, h_send, s_send, p_sems,
):
    z, f = lax.axis_index("wa"), lax.axis_index("facet")
    core = f % 2
    seat = 2 * z + core
    pair = f - core

    def at(other_seat):
        return (other_seat // 2, pair + other_seat % 2)

    def is_seat(*seats):
        hit = seat == seats[0]
        for other in seats[1:]:
            hit = jnp.logical_or(hit, seat == other)
        return hit

    barrier = pltpu.get_barrier_semaphore()
    for step in range(1, 8):
        pl.semaphore_signal(barrier, inc=1, device_id=at((seat + step) % 8), device_id_type=MESH)

    for tile in range(GRID // SUB):
        rows = row_ref[pl.ds(tile * SUB, SUB), :]
        col[pl.ds(tile * 128, SUB), :] = rows
        col[pl.ds(tile * 128 + SUB, SUB), pl.ds(0, GRID)] = -rows[:, GRID:]
        col[pl.ds(tile * 128 + SUB, SUB), pl.ds(GRID, GRID)] = rows[:, :GRID]

    pl.semaphore_wait(barrier, 7)

    partner = at(seat + 1 - 2 * core)
    gives = is_seat(0, 2, 5)
    takes = is_seat(1, 3, 4)

    def phase_out():
        return pltpu.make_async_remote_copy(
            src_ref=phase_ref, dst_ref=phase, send_sem=p_sems.at[0], recv_sem=p_sems.at[1],
            device_id=partner, device_id_type=MESH,
        )

    def phase_own():
        return pltpu.make_async_copy(phase_ref, phase, p_sems.at[2])

    @pl.when(gives)
    def _():
        phase_out().start()

    @pl.when(jnp.logical_not(takes))
    def _():
        phase_own().start()
        phase_own().wait()

    @pl.when(takes)
    def _():
        phase_out().wait_recv()

    to_h = jnp.where(seat == 5, 4, jnp.where(seat == 7, 5, seat + 1))
    sends_h = is_seat(0, 1, 2, 5, 6, 7)
    takes_h = is_seat(1, 2, 3, 4, 5, 7)
    to_s = jnp.where(seat == 0, 6, jnp.where(seat == 2, 4, jnp.where(seat == 3, 0,
           jnp.where(seat == 4, 7, jnp.where(seat == 5, 3, 1)))))
    takes_s = is_seat(0, 1, 3, 4, 6, 7)

    def copy_h(i):
        rows = pl.ds(pl.multiple_of(i * CHUNK, CHUNK), CHUNK)
        return pltpu.make_async_remote_copy(
            src_ref=mine.at[rows], dst_ref=from_h.at[rows], send_sem=h_send.at[i], recv_sem=h_recv.at[i],
            device_id=at(to_h), device_id_type=MESH,
        )

    def copy_s(i, source):
        rows = pl.ds(pl.multiple_of(i * CHUNK, CHUNK), CHUNK)
        return pltpu.make_async_remote_copy(
            src_ref=source.at[rows], dst_ref=from_s.at[rows], send_sem=s_send.at[i], recv_sem=s_recv.at[i],
            device_id=at(to_s), device_id_type=MESH,
        )

    def work(i, carry):
        rows = pl.ds(pl.multiple_of(i * CHUNK, CHUNK), CHUNK)
        half = jnp.dot(row_ref[rows, :], gj_ref[...], preferred_element_type=F32).astype(BF16)
        image = jnp.dot(half, col[...], preferred_element_type=F32)

        @pl.when(takes_h)
        def _():
            copy_h(i).wait_recv()

            @pl.when(seat == 5)
            def _():
                copy_s(i, from_h).start()

            p_re, p_im = sincos(phase[rows, :])
            f_re = from_h[rows, pl.ds(0, GRID)].astype(F32)
            f_im = from_h[rows, pl.ds(GRID, GRID)].astype(F32)
            mine[rows, pl.ds(0, GRID)] = (p_re * f_re - p_im * f_im + image[:, :GRID]).astype(BF16)
            mine[rows, pl.ds(GRID, GRID)] = (p_re * f_im + p_im * f_re + image[:, GRID:]).astype(BF16)

        @pl.when(jnp.logical_not(takes_h))
        def _():
            mine[rows, :] = image.astype(BF16)

        @pl.when(sends_h)
        def _():
            copy_h(i).start()

        @pl.when(is_seat(2, 3, 4, 6))
        def _():
            copy_s(i, mine).start()

        @pl.when(is_seat(0, 5))
        def _():
            out_ref[rows, :] = mine[rows, :]

        @pl.when(seat == 2)
        def _():
            out_ref[rows, :] = from_h[rows, :]

        return carry

    lax.fori_loop(0, CHUNKS, work, 0)

    def finish(i, carry):
        rows = pl.ds(pl.multiple_of(i * CHUNK, CHUNK), CHUNK)

        @pl.when(takes_s)
        def _():
            copy_s(i, mine).wait_recv()

        @pl.when(seat == 0)
        def _():
            copy_s(i, from_s).start()

        @pl.when(is_seat(1, 3, 4, 6, 7))
        def _():
            out_ref[rows, :] = from_s[rows, :]

        return carry

    lax.fori_loop(0, CHUNKS, finish, 0)

    @pl.when(gives)
    def _():
        phase_out().wait_send()

    def drain(i, carry):
        @pl.when(sends_h)
        def _():
            copy_h(i).wait_send()

        @pl.when(is_seat(0, 2, 3, 4, 5, 6))
        def _():
            copy_s(i, mine).wait_send()

        return carry

    lax.fori_loop(0, CHUNKS, drain, 0)


def chain(gj, row_table, phase):
    return pl.pallas_call(
        chain_kernel,
        out_shape=jax.ShapeDtypeStruct((GRID, 2 * GRID), BF16),
        in_specs=[VMEM, VMEM, pl.BlockSpec(memory_space=pl.ANY)],
        out_specs=VMEM,
        scratch_shapes=[
            pltpu.VMEM((2 * GRID, 2 * GRID), BF16),
            pltpu.VMEM((GRID, GRID), F32),
            pltpu.VMEM((GRID, 2 * GRID), BF16),
            pltpu.VMEM((GRID, 2 * GRID), BF16),
            pltpu.VMEM((GRID, 2 * GRID), BF16),
            pltpu.SemaphoreType.DMA((CHUNKS,)),
            pltpu.SemaphoreType.DMA((CHUNKS,)),
            pltpu.SemaphoreType.DMA((CHUNKS,)),
            pltpu.SemaphoreType.DMA((CHUNKS,)),
            pltpu.SemaphoreType.DMA((3,)),
        ],
        compiler_params=pltpu.CompilerParams(collective_id=1, has_side_effects=True),
        name="chain",
    )(gj, row_table, phase)


def dft_rows():
    line = np.arange(GRID)
    angle = (line[:, None] * line[None, :] % GRID) * (2.0 * math.pi / GRID)
    table = np.concatenate([np.cos(angle), np.sin(angle)], axis=1) / math.sqrt(GRID)
    return table.astype(np.float32).astype(ml_dtypes.bfloat16)


def on_device(visibilities, uv_angles, routes, offsets, pixel_phase):
    vis = visibilities.transpose(1, 2, 0).reshape(2 * NVIS, SUBS)
    ang = uv_angles.transpose(1, 2, 0).reshape(2 * NVIS, SUBS)
    send = pack(vis, ang, routes.reshape(1, SUBS), offsets.T)
    recv = lax.all_to_all(
        send.reshape(SUBS, ROWS, 128), ("wa", "facet"), split_axis=0, concat_axis=0, tiled=True
    )
    gj = grid_owner(recv.reshape(SUBS * ROWS, 128))
    result = chain(gj, jnp.asarray(dft_rows()), pixel_phase[0])
    return result.astype(F32).reshape(1, 1, GRID, 2 * GRID)


def solution(mesh):
    in_specs = (
        P(("wa", "facet"), None, None),
        P(("wa", "facet"), None, None),
        P(("wa", "facet"), None),
        P(("wa", "facet"), None),
        P("facet", None, None),
    )
    out_specs = P("wa", "facet", None, None)
    return jax.shard_map(
        on_device, mesh=mesh, in_specs=in_specs, out_specs=out_specs, check_vma=False
    )
```

time: 563 us -> 74.1 us (0.13)
  the two profiles are of different devices: /device:TPU:1 before, /device:TPU:0 now
where the time goes in v1:
time: 74.1 us; the launch traced here: 73.8 us
  Pallas kernels  49 us (66%)
  blocking collectives  22 us (30%)
  other arithmetic  2.79 us (4%)
    pallas_call x1, Pallas kernels, chain(): pl.pallas_call(chain_kernel, out_shape=jax.ShapeDtypeStruct((GRID, 2 * GR...  29 us
    all_to_all x1, blocking collectives, on_device(): lax.all_to_all(send.reshape(SUBS, ROWS, 128), ('wa', 'facet'), split_axis...  22 us
    pallas_call x1, Pallas kernels, grid_owner(): pl.pallas_call(grid_kernel, out_shape=jax.ShapeDtypeStruct((2 * GRID, 2 *...  17.8 us
    reshape x1, other arithmetic, on_device(): return result.astype(F32).reshape(1, 1, GRID, 2 * GRID)  2.79 us
    pallas_call x1, Pallas kernels, pack(): pl.pallas_call(pack_kernel, out_shape=jax.ShapeDtypeStruct((SUBS * ROWS,...  2.19 us

profile of v1, /device:TPU:0, one launch (start us, length us, event | category | flops | bytes accessed | tf_op | source)
XLA Modules:
  0.0 73.8 jit_solution(15764862511733501646)
XLA Ops:
  0.0 2.2 %pack.1 = bf16[1024,128]{1,0:T(8,128)(2,1)} custom-call(bf16[128,128]{1,0:T(8,128)(2,1)} %bitcast.18, f32[128,128]{1,0:T(8,128)} %bitcast.17, s32[1,128]{1,0:T(1,128)} %bitcast.20, s32[2,128]{1,0:T(2,128)} %bitcast.19), custom_call_target="tpu_custom_call" | custom-call | tf_op jit(solution)/shard_map/pack/pallas_call | solution.py:90
  2.2 22.0 %all_to_all.5 = bf16[128,8,128]{2,1,0:T(8,128)(2,1)} all-to-all(bf16[128,8,128]{2,1,0:T(8,128)(2,1)} %bitcast.16), channel_id=1, replica_groups=mesh['wa'=4,'facet'=32] {'wa','facet'}, dimensions={0} | all-to-all | bytes 524288 | tf_op jit(solution)/shard_map/all_to_all | solution.py:441
  24.2 17.8 %grid.1.gj_ref = bf16[1024,1024]{1,0:T(8,128)(2,1)} custom-call(bf16[1024,128]{1,0:T(8,128)(2,1)} %bitcast.15), custom_call_target="tpu_custom_call" | custom-call | tf_op jit(solution)/shard_map/grid/pallas_call | solution.py:232
  42.0 29.0 %chain.1 = bf16[512,1024]{1,0:T(8,128)(2,1)} custom-call(bf16[1024,1024]{1,0:T(8,128)(2,1)} %grid.1.gj_ref, bf16[512,1024]{1,0:T(8,128)(2,1)} %constant.2.clone.row_ref, f32[512,512]{1,0:T(8,128)} %bitcast.14), custom_call_target="tpu_custom_call" | custom-call | tf_op jit(solution)/shard_map/chain/pallas_call | solution.py:408
  71.0 2.8 %bitcast_convert_fusion = f32[1,1,512,1024]{3,2,1,0:T(8,128)} fusion(bf16[512,1024]{1,0:T(8,128)(2,1)} %chain.1), kind=kLoop, calls=%fused_computation | loop fusion | flops 524288 | bytes 3145728 | tf_op jit(solution)/shard_map/reshape | solution.py:446

commit v2 on v1

v2 whole, which is shorter than its diff:
```python
import functools
import math

import jax
import jax.numpy as jnp
import ml_dtypes
import numpy as np
from jax import lax
from jax.experimental import pallas as pl
from jax.experimental.pallas import tpu as pltpu
from jax.sharding import PartitionSpec as P

SUB = 64
GRID = 512
NVIS = 64
SUBS = 128
CAP = 2
KINDS = 4
ROWS = CAP * KINDS
BLOCK = 64
CHUNK = 32
CHUNKS = GRID // CHUNK
UNROLL = 4
BF16 = jnp.bfloat16
F32 = jnp.float32
MESH = pl.DeviceIdType.MESH
VMEM = pl.BlockSpec(memory_space=pltpu.VMEM)
NT = (((1,), (1,)), ((), ()))


def sincos(x):
    h = x * 0.5
    q = h * h
    s = h + h * q * (
        -1.6666666666666602e-1
        + q * (8.333333333320001e-3
        + q * (-1.9841269829589539e-4
        + q * (2.7557314297030280e-6
        + q * (-2.5050747762850355e-8
        + q * 1.5891812000000000e-10))))
    )
    c = 1.0 + q * (
        -0.5
        + q * (4.16666666666665929218e-2
        + q * (-1.38888888888730564116e-3
        + q * (2.48015872888517045348e-5
        + q * (-2.75573141792967388112e-7
        + q * 2.08757008419747316778e-9))))
    )
    return 1.0 - 2.0 * s * s, 2.0 * s * c


def route_kernel(vis_ref, ang_ref, route_ref, off_ref, out_ref, send, recv, send_sem, recv_sem):
    z, f = lax.axis_index("wa"), lax.axis_index("facet")
    x, y, core = f >> 3, (f >> 1) & 3, f & 1
    me = z * 32 + f

    def peer(k):
        def far_first(n):
            return jnp.where(n == 0, 2, jnp.where(n == 3, 0, jnp.where(n == 1, 1, 3)))

        z_to = (z + far_first(k >> 5)) & 3
        x_to = (x + far_first((k >> 3) & 3)) & 3
        y_to = (y + far_first((k >> 1) & 3)) & 3
        return z_to, (x_to << 3) | (y_to << 1) | (core ^ (k & 1) ^ 1)

    barrier = pltpu.get_barrier_semaphore()

    def greet(k, carry):
        pl.semaphore_signal(barrier, inc=1, device_id=peer(k), device_id_type=MESH)
        return carry

    lax.fori_loop(0, SUBS - 1, greet, 0)

    owner = route_ref[...]
    facet = owner & 31
    plane = owner >> 5
    odd = facet & 1
    seat = jnp.where(odd == 1, 6, 0)
    seat = jnp.where(plane == 1, jnp.where(odd == 1, 4, 2), seat)
    seat = jnp.where(plane == 2, jnp.where(odd == 1, 5, 3), seat)
    seat = jnp.where(plane == 3, jnp.where(odd == 1, 7, 1), seat)
    device = ((seat >> 1) << 5) + (facet - odd) + (seat & 1)
    owner_b = jnp.broadcast_to(owner.astype(F32), (SUBS, SUBS))
    row_i = lax.broadcasted_iota(jnp.int32, (SUBS, SUBS), 0)
    col_i = lax.broadcasted_iota(jnp.int32, (SUBS, SUBS), 1)
    earlier = jnp.where((owner_b == owner_b.T) & (row_i < col_i), 1.0, 0.0)
    rank = jnp.sum(earlier, axis=0, keepdims=True).astype(jnp.int32)
    slot = device * CAP + rank
    total = SUBS * CAP
    col_key = jnp.concatenate([slot + kind * total for kind in range(KINDS)], axis=1)

    angle = ang_ref[...]
    high = angle.astype(BF16)
    low = (angle - high.astype(F32)).astype(BF16)
    off_u, off_v = off_ref[0:1, :], off_ref[1:2, :]
    meta = jnp.where(row_i == 0, off_u >> 4, 0)
    meta = jnp.where(row_i == 1, off_u & 15, meta)
    meta = jnp.where(row_i == 2, off_v >> 4, meta)
    meta = jnp.where(row_i == 3, off_v & 15, meta)
    meta = meta.astype(F32).astype(BF16)
    data = jnp.concatenate([high, low, vis_ref[...], meta], axis=1)

    for block in range(ROWS):
        row = lax.broadcasted_iota(jnp.int32, (SUBS, KINDS * SUBS), 0) + block * SUBS
        place = row & (ROWS - 1)
        row_key = (place // CAP) * total + (row // ROWS) * CAP + place % CAP
        one_hot = jnp.where(row_key == col_key, 1.0, 0.0).astype(BF16)
        picked = lax.dot_general(one_hot, data, NT, preferred_element_type=F32)
        per = SUBS // ROWS
        send[pl.ds(block * per, per)] = picked.astype(BF16).reshape(per, ROWS, 128)

    pl.semaphore_wait(barrier, SUBS - 1)

    def post(k, carry):
        z_to, f_to = peer(k)
        pltpu.make_async_remote_copy(
            src_ref=send.at[z_to * 32 + f_to], dst_ref=recv.at[me], send_sem=send_sem, recv_sem=recv_sem,
            device_id=(z_to, f_to), device_id_type=MESH,
        ).start()
        return carry

    lax.fori_loop(0, SUBS - 1, post, 0)
    recv[me] = send[me]
    others = pl.ds(0, SUBS - 1)
    pltpu.make_async_copy(send.at[others], recv.at[others], recv_sem).wait()
    out_ref[...] = recv[...]
    pltpu.make_async_copy(send.at[others], recv.at[others], send_sem).wait()


def route(vis, ang, owners, off):
    return pl.pallas_call(
        route_kernel,
        out_shape=jax.ShapeDtypeStruct((SUBS, ROWS, 128), BF16),
        in_specs=[VMEM] * 4,
        out_specs=VMEM,
        scratch_shapes=[
            pltpu.VMEM((SUBS, ROWS, 128), BF16),
            pltpu.VMEM((SUBS, ROWS, 128), BF16),
            pltpu.SemaphoreType.DMA,
            pltpu.SemaphoreType.DMA,
        ],
        compiler_params=pltpu.CompilerParams(
            collective_id=0, has_side_effects=True, vmem_limit_bytes=8 << 20
        ),
        name="route",
    )(vis, ang, owners, off)


def complex_mul(a, b):
    return a[0] * b[0] - a[1] * b[1], a[0] * b[1] + a[1] * b[0]


def grid_kernel(
    recv_ref, grid_ref, wide, pos_v, pos_s, pos_sem, au_r, au_i, av_r, av_i, bu, bv, acc_a, acc_b, sub_a, sub_b
):
    slots = SUBS * CAP
    wide[...] = recv_ref[...].astype(F32)

    lane8 = lax.broadcasted_iota(jnp.int32, (8, 128), 1)
    weight = jnp.where(lane8 == 0, 8192.0, 0.0)
    weight = jnp.where(lane8 == 1, 512.0, weight)
    weight = jnp.where(lane8 == 2, 16.0, weight)
    weight = jnp.where(lane8 == 3, 1.0, weight).astype(BF16)
    for j in range(CAP):
        meta = wide[pl.ds((KINDS - 1) * CAP + j, SUBS, stride=ROWS), :].astype(BF16)
        packed = lax.dot_general(weight, meta, NT, preferred_element_type=F32)
        pos_v[j] = packed.astype(jnp.int32)
    to_scalar = pltpu.make_async_copy(pos_v, pos_s, pos_sem)
    to_scalar.start()

    acc_a[...] = jnp.zeros_like(acc_a)
    acc_b[...] = jnp.zeros_like(acc_b)
    sub_b[...] = jnp.zeros_like(sub_b)

    group = 16
    first = lax.broadcasted_iota(jnp.int32, (group, 128), 1) < 64

    def tables(g, carry):
        for j in range(CAP):
            start = g * group

            def rows(kind):
                at = start * ROWS + kind * CAP + j
                return wide[pl.ds(at, group, stride=ROWS), :]

            cos_t, sin_t = sincos(rows(0) + rows(1))
            vis = rows(2) * (1.0 / math.sqrt(NVIS))
            cos_o, sin_o = pltpu.roll(cos_t, 64, 1), pltpu.roll(sin_t, 64, 1)
            vis_o = pltpu.roll(vis, 64, 1)
            vis2 = (vis, jnp.where(first, vis_o, -vis_o))
            slot = pl.multiple_of(start + j * SUBS, group)
            for side in range(2):
                if side == 0:
                    e1 = (jnp.where(first, cos_t, cos_o), jnp.where(first, sin_t, sin_o))
                else:
                    e1 = (jnp.where(first, cos_o, cos_t), jnp.where(first, sin_o, sin_t))
                e2 = complex_mul(e1, e1)
                e3 = complex_mul(e2, e1)
                e4 = complex_mul(e2, e2)
                e5 = complex_mul(e4, e1)
                e6 = complex_mul(e4, e2)
                e7 = complex_mul(e4, e3)
                e8 = complex_mul(e4, e4)
                e16 = complex_mul(e8, e8)
                e24 = complex_mul(e16, e8)
                e32 = complex_mul(e16, e16)
                one = (jnp.ones_like(cos_t), jnp.zeros_like(cos_t))
                for a, e in enumerate((one, e1, e2, e3, e4, e5, e6, e7)):
                    where = pl.ds(slot * 8 + a, group, stride=8)
                    if side == 0:
                        re, im = complex_mul(e, vis2)
                        au_r[where, :] = re
                        au_i[where, :] = im
                    else:
                        av_r[where, :] = jnp.where(first, e[0], -e[1])
                        av_i[where, :] = jnp.where(first, e[1], e[0])
                steps = bu if side == 0 else bv
                for b, e in enumerate((e8, e16, e24, e32)):
                    steps[2 * b, pl.ds(slot, group), :] = e[0]
                    steps[2 * b + 1, pl.ds(slot, group), :] = e[1]
        return carry

    lax.fori_loop(0, SUBS // group, tables, 0)
    to_scalar.wait()

    lane_in = lax.broadcasted_iota(jnp.int32, (SUB, 128), 1) & 63

    def form(slot):
        base = pl.multiple_of(slot * 8, 8)
        ur, ui = au_r[pl.ds(base, 8), :], au_i[pl.ds(base, 8), :]
        vr, vi = av_r[pl.ds(base, 8), :], av_i[pl.ds(base, 8), :]

        def step(table, b):
            return table[2 * b, pl.ds(slot, 1), :], table[2 * b + 1, pl.ds(slot, 1), :]

        left = [None] * 8
        right_r = [None] * 8
        right_i = [None] * 8
        left[4], right_r[4], right_i[4] = ur, vr, vi
        for b in range(4):
            br, bi = step(bu, b)
            x, y = br * ur, bi * ui
            left[3 - b] = x + y
            if b < 3:
                left[5 + b] = x - y
            br, bi = step(bv, b)
            x, y, z, w = br * vr, bi * vi, br * vi, bi * vr
            right_r[3 - b] = x + y
            right_i[3 - b] = z - w
            if b < 3:
                right_r[5 + b] = x - y
                right_i[5 + b] = z + w
        left = jnp.concatenate(left, axis=0).astype(BF16)
        right = jnp.concatenate(right_r + right_i, axis=0).astype(BF16)
        return lax.dot_general(left, right, NT, preferred_element_type=F32)

    def place(slot, sub, acc):
        packed = pos_s[slot >> 7, 0, slot & (SUBS - 1)]
        off_u, off_v = packed >> 9, packed & 511
        tile, shift = off_v >> 6, off_v & 63
        turned = pltpu.roll(sub, shift, 1)
        rows = pl.ds(off_u, SUB)
        here, there = acc.at[tile, rows, :], acc.at[tile + 1, rows, :]
        near = here[...] + turned
        far = there[...] + pltpu.roll(turned, 64, 1)
        pltpu.store(here, near, mask=lane_in >= shift)
        pltpu.store(there, far, mask=lane_in < shift)

    def work(i, carry):
        now = i * (2 * UNROLL)
        before = jnp.maximum(now - UNROLL, 0)
        for n in range(UNROLL):
            sub_a[n] = form(now + n)
        for n in range(UNROLL):
            place(before + n, sub_b[n], (acc_a, acc_b)[n % 2])
        for n in range(UNROLL):
            sub_b[n] = form(now + UNROLL + n)
        for n in range(UNROLL):
            place(now + n, sub_a[n], (acc_a, acc_b)[n % 2])
        return carry

    lax.fori_loop(0, slots // (2 * UNROLL), work, 0)
    for n in range(UNROLL):
        place(slots - UNROLL + n, sub_b[n], (acc_a, acc_b)[n % 2])

    for tile in range(GRID // SUB):
        grid_ref[:, pl.ds(tile * 128, 128)] = (acc_a[tile] + acc_b[tile]).astype(BF16)


def grid_owner(recv):
    slots = SUBS * CAP
    return pl.pallas_call(
        grid_kernel,
        out_shape=jax.ShapeDtypeStruct((GRID, 2 * GRID), BF16),
        in_specs=[VMEM],
        out_specs=VMEM,
        scratch_shapes=[
            pltpu.VMEM((SUBS * ROWS, 128), F32),
            pltpu.VMEM((CAP, 8, 128), jnp.int32),
            pltpu.SMEM((CAP, 8, 128), jnp.int32),
            pltpu.SemaphoreType.DMA,
        ]
        + [pltpu.VMEM((slots * 8, 128), F32)] * 4
        + [pltpu.VMEM((8, slots, 128), F32)] * 2
        + [pltpu.VMEM((GRID // SUB + 1, GRID, 128), F32)] * 2
        + [pltpu.VMEM((UNROLL, SUB, 128), F32)] * 2,
        compiler_params=pltpu.CompilerParams(vmem_limit_bytes=22 << 20),
        name="grid",
    )(recv)


def chain_kernel(
    grid_ref, row_ref, phase_ref, out_ref, col, phase, p_re, p_im, image, from_h, from_s, mine,
    h_recv, s_recv, h_send, s_send, p_sems,
):
    z, f = lax.axis_index("wa"), lax.axis_index("facet")
    core = f & 1
    seat = 2 * z + core
    pair = f - core

    def at(other_seat):
        return (other_seat >> 1, pair + (other_seat & 1))

    def is_seat(*seats):
        hit = seat == seats[0]
        for other in seats[1:]:
            hit = jnp.logical_or(hit, seat == other)
        return hit

    barrier = pltpu.get_barrier_semaphore()
    for step in range(1, 8):
        pl.semaphore_signal(barrier, inc=1, device_id=at((seat + step) & 7), device_id_type=MESH)

    gives = is_seat(0, 2, 5)
    takes = is_seat(1, 3, 4)
    keeps = is_seat(2, 5, 7)

    def phase_out():
        return pltpu.make_async_remote_copy(
            src_ref=phase_ref, dst_ref=phase, send_sem=p_sems.at[0], recv_sem=p_sems.at[1],
            device_id=at(seat ^ 1), device_id_type=MESH,
        )

    def phase_own():
        return pltpu.make_async_copy(phase_ref, phase, p_sems.at[2])

    @pl.when(keeps)
    def _():
        phase_own().start()

    for tile in range(GRID // SUB):
        rows = row_ref[pl.ds(tile * SUB, SUB), :]
        col[pl.ds(tile * 128, SUB), :] = rows
        col[pl.ds(tile * 128 + SUB, SUB), pl.ds(0, GRID)] = -rows[:, GRID:]
        col[pl.ds(tile * 128 + SUB, SUB), pl.ds(GRID, GRID)] = rows[:, :GRID]

    pl.semaphore_wait(barrier, 7)

    @pl.when(gives)
    def _():
        phase_out().start()

    to_h = jnp.where(seat == 0, 2, jnp.where(seat == 2, 3, jnp.where(seat == 3, 1,
           jnp.where(seat == 6, 4, jnp.where(seat == 4, 5, 7)))))
    to_s = jnp.where(seat == 1, 6, jnp.where(seat == 3, 4, jnp.where(seat == 4, 3, 1)))
    sends_h = is_seat(0, 2, 3, 4, 5, 6)
    takes_h = is_seat(1, 2, 3, 4, 5, 7)
    away = is_seat(1, 3, 4, 6)

    def chunk_rows(i):
        return pl.ds(pl.multiple_of(i * CHUNK, CHUNK), CHUNK)

    def copy_h(i):
        rows = chunk_rows(i)
        return pltpu.make_async_remote_copy(
            src_ref=mine.at[rows], dst_ref=from_h.at[rows], send_sem=h_send.at[i], recv_sem=h_recv.at[i],
            device_id=at(to_h), device_id_type=MESH,
        )

    def copy_s(i):
        rows = chunk_rows(i)
        return pltpu.make_async_remote_copy(
            src_ref=mine.at[rows], dst_ref=from_s.at[rows], send_sem=s_send.at[i], recv_sem=s_recv.at[i],
            device_id=at(to_s), device_id_type=MESH,
        )

    real = lax.broadcasted_iota(jnp.int32, (BLOCK, 2 * GRID), 1) & 127 < 64

    def work(i, carry):
        rows = pl.ds(pl.multiple_of(i * BLOCK, BLOCK), BLOCK)
        both = jnp.concatenate([row_ref[rows, pl.ds(0, GRID)], row_ref[rows, pl.ds(GRID, GRID)]], axis=0)
        parts = jnp.dot(both, grid_ref[...], preferred_element_type=F32)
        turned = jnp.concatenate(
            [pltpu.roll(parts[BLOCK:, t * 128 : (t + 1) * 128], 64, 1) for t in range(GRID // SUB)], axis=1
        )
        half = parts[:BLOCK] + jnp.where(real, -turned, turned)
        image[...] = jnp.dot(half.astype(BF16), col[...], preferred_element_type=F32)

        @pl.when(takes_h)
        def _():
            @pl.when(i == 0)
            def _():
                @pl.when(takes)
                def _():
                    phase_out().wait_recv()

                @pl.when(keeps)
                def _():
                    phase_own().wait()

            c, s = sincos(phase[rows, :])
            p_re[...] = c
            p_im[...] = s

        for part in range(BLOCK // CHUNK):
            chunk = i * (BLOCK // CHUNK) + part
            at_rows = chunk_rows(chunk)
            local = pl.ds(part * CHUNK, CHUNK)

            @pl.when(takes_h)
            def _():
                copy_h(chunk).wait_recv()
                f_re = from_h[at_rows, pl.ds(0, GRID)].astype(F32)
                f_im = from_h[at_rows, pl.ds(GRID, GRID)].astype(F32)
                c, s = p_re[local, :], p_im[local, :]
                im_re, im_im = image[local, pl.ds(0, GRID)], image[local, pl.ds(GRID, GRID)]
                mine[at_rows, pl.ds(0, GRID)] = (c * f_re - s * f_im + im_re).astype(BF16)
                mine[at_rows, pl.ds(GRID, GRID)] = (c * f_im + s * f_re + im_im).astype(BF16)

            @pl.when(jnp.logical_not(takes_h))
            def _():
                mine[at_rows, :] = image[local, :].astype(BF16)

            @pl.when(sends_h)
            def _():
                copy_h(chunk).start()

            @pl.when(away)
            def _():
                copy_s(chunk).start()

            @pl.when(jnp.logical_not(away))
            def _():
                out_ref[at_rows, :] = mine[at_rows, :]

        return carry

    lax.fori_loop(0, GRID // BLOCK, work, 0)

    @pl.when(away)
    def _():
        def finish(i, carry):
            copy_s(i).wait_recv()
            out_ref[chunk_rows(i), :] = from_s[chunk_rows(i), :]
            return carry

        lax.fori_loop(0, CHUNKS, finish, 0)

    @pl.when(gives)
    def _():
        phase_out().wait_send()

    def drain(i, carry):
        @pl.when(sends_h)
        def _():
            copy_h(i).wait_send()

        @pl.when(away)
        def _():
            copy_s(i).wait_send()

        return carry

    lax.fori_loop(0, CHUNKS, drain, 0)


def chain(grid, row_table, phase):
    band = (GRID, 2 * GRID)
    return pl.pallas_call(
        chain_kernel,
        out_shape=jax.ShapeDtypeStruct(band, BF16),
        in_specs=[VMEM, VMEM, pl.BlockSpec(memory_space=pl.ANY)],
        out_specs=VMEM,
        scratch_shapes=[
            pltpu.VMEM((2 * GRID, 2 * GRID), BF16),
            pltpu.VMEM((GRID, GRID), F32),
            pltpu.VMEM((BLOCK, GRID), F32),
            pltpu.VMEM((BLOCK, GRID), F32),
            pltpu.VMEM((BLOCK, 2 * GRID), F32),
            pltpu.VMEM(band, BF16),
            pltpu.VMEM(band, BF16),
            pltpu.VMEM(band, BF16),
        ]
        + [pltpu.SemaphoreType.DMA((CHUNKS,))] * 4
        + [pltpu.SemaphoreType.DMA((3,))],
        compiler_params=pltpu.CompilerParams(
            collective_id=1, has_side_effects=True, vmem_limit_bytes=18 << 20
        ),
        name="chain",
    )(grid, row_table, phase)


def dft_rows():
    line = np.arange(GRID)
    angle = (line[:, None] * line[None, :] % GRID) * (2.0 * math.pi / GRID)
    table = np.concatenate([np.cos(angle), np.sin(angle)], axis=1) / math.sqrt(GRID)
    return table.astype(np.float32).astype(ml_dtypes.bfloat16)


def on_device(visibilities, uv_angles, routes, offsets, pixel_phase):
    vis = visibilities.transpose(1, 2, 0).reshape(2 * NVIS, SUBS)
    ang = uv_angles.transpose(1, 2, 0).reshape(2 * NVIS, SUBS)
    recv = route(vis, ang, routes.reshape(1, SUBS), offsets.T)
    grid = grid_owner(recv.reshape(SUBS * ROWS, 128))
    result = chain(grid, jnp.asarray(dft_rows()), pixel_phase[0])
    return result.astype(F32).reshape(1, 1, GRID, 2 * GRID)


def solution(mesh):
    in_specs = (
        P(("wa", "facet"), None, None),
        P(("wa", "facet"), None, None),
        P(("wa", "facet"), None),
        P(("wa", "facet"), None),
        P("facet", None, None),
    )
    out_specs = P("wa", "facet", None, None)
    return jax.shard_map(
        on_device, mesh=mesh, in_specs=in_specs, out_specs=out_specs, check_vma=False
    )
```

time: 74.1 us -> 60.4 us (0.82)
  the two profiles are of different devices: /device:TPU:0 before, /device:TPU:1 now
where the time goes in v2:
time: 60.4 us; the launch traced here: 60.2 us
  Pallas kernels  54.4 us (90%)
  local copies, waits for them, and re-layouts  4.24 us (7%)
  other arithmetic  1.57 us (3%)
    pallas_call x1, Pallas kernels, chain(): pl.pallas_call(chain_kernel, out_shape=jax.ShapeDtypeStruct(band, BF16),...  22.7 us
    pallas_call x1, Pallas kernels, route(): pl.pallas_call(route_kernel, out_shape=jax.ShapeDtypeStruct((SUBS, ROWS,...  16.9 us
    pallas_call x1, Pallas kernels, grid_owner(): pl.pallas_call(grid_kernel, out_shape=jax.ShapeDtypeStruct((GRID, 2 * GRI...  14.8 us
    unnamed x12, local copies, waits for them, and re-layouts  4.24 us
    reshape x1, other arithmetic, on_device(): return result.astype(F32).reshape(1, 1, GRID, 2 * GRID)  1.57 us

profile of v2, /device:TPU:1, one launch (start us, length us, event | category | flops | bytes accessed | tf_op | source)
XLA Modules:
  0.0 60.2 jit_solution(10872968530428936937)
XLA Ops:
  0.0 0.0 copy-start
  0.0 0.0 copy-start.2
  0.0 0.9 %copy-done.2 = f32[128,2,64]{0,2,1:T(8,128)S(1)} copy-done((f32[128,2,64]{0,2,1:T(8,128)S(1)}, f32[128,2,64]{0,2,1:T(8,128)}, u32[]{:S(2)}) %copy-start.2) | copy-done | bytes 65560
  0.9 0.0 copy-start.3
  0.9 0.8 %copy-done.3 = bf16[128,2,64]{0,2,1:T(8,128)(2,1)S(1)} copy-done((bf16[128,2,64]{0,2,1:T(8,128)(2,1)S(1)}, bf16[128,2,64]{0,2,1:T(8,128)(2,1)}, u32[]{:S(2)}) %copy-start.3) | copy-done | bytes 32792
  1.7 0.0 copy-start.4
  1.7 0.7 %copy-done.4 = s32[128,2]{0,1:T(2,128)S(1)} copy-done((s32[128,2]{0,1:T(2,128)S(1)}, s32[128,2]{0,1:T(2,128)}, u32[]{:S(2)}) %copy-start.4) | copy-done | bytes 1048
  2.4 0.0 copy-start.5
  2.4 0.7 %copy-done.5 = s32[128,1]{0,1:T(1,128)S(1)} copy-done((s32[128,1]{0,1:T(1,128)S(1)}, s32[128,1]{0,1:T(1,128)}, u32[]{:S(2)}) %copy-start.5) | copy-done | bytes 536
  3.0 16.9 %route.1 = bf16[128,8,128]{2,1,0:T(8,128)(2,1)S(1)} custom-call(bf16[128,128]{1,0:T(8,128)(2,1)S(1)} %bitcast.16, f32[128,128]{1,0:T(8,128)S(1)} %bitcast.15, s32[1,128]{1,0:T(1,128)S(1)} %bitcast.18, s32[2,128]{1,0:T(2,128)S(1)} %bitcast.17), custom_call_target="tpu_custom_call" | custom-call | tf_op jit(solution)/shard_map/route/pallas_call | solution.py:132
  19.9 14.8 %grid.1.grid_ref = bf16[512,1024]{1,0:T(8,128)(2,1)S(1)} custom-call(bf16[1024,128]{1,0:T(8,128)(2,1)S(1)} %bitcast.13), custom_call_target="tpu_custom_call" | custom-call | tf_op jit(solution)/shard_map/grid/pallas_call | solution.py:293
  34.7 0.0 copy-done
  34.7 0.0 copy-start.1
  34.8 1.2 %copy-done.1 = bf16[512,1024]{1,0:T(8,128)(2,1)S(1)} copy-done((bf16[512,1024]{1,0:T(8,128)(2,1)S(1)}, bf16[512,1024]{1,0:T(8,128)(2,1)}, u32[]{:S(2)}) %copy-start.1) | copy-done | bytes 1048600
  36.0 22.7 %chain.1 = bf16[512,1024]{1,0:T(8,128)(2,1)S(1)} custom-call(bf16[512,1024]{1,0:T(8,128)(2,1)S(1)} %grid.1.grid_ref, bf16[512,1024]{1,0:T(8,128)(2,1)S(1)} %copy-done.1, f32[512,512]{1,0:T(8,128)S(1)} %bitcast.14), custom_call_target="tpu_custom_call" | custom-call | tf_op jit(solution)/shard_map/chain/pallas_call | solution.py:480
  58.6 1.6 %bitcast_convert_fusion = f32[1,1,512,1024]{3,2,1,0:T(8,128)} fusion(bf16[512,1024]{1,0:T(8,128)(2,1)S(1)} %chain.1), kind=kLoop, calls=%fused_computation | loop fusion | flops 524288 | bytes 3145728 | tf_op jit(solution)/shard_map/reshape | solution.py:517
Async XLA Ops:
  0.0 34.7 %copy-start = (f32[1,512,512]{2,1,0:T(8,128)S(1)}, f32[1,512,512]{2,1,0:T(8,128)}, u32[]{:S(2)}) copy-start(f32[1,512,512]{2,1,0:T(8,128)} %param.10) | copy-start | bytes 3145732
  0.0 0.9 %copy-start.2 = (f32[128,2,64]{0,2,1:T(8,128)S(1)}, f32[128,2,64]{0,2,1:T(8,128)}, u32[]{:S(2)}) copy-start(f32[128,2,64]{0,2,1:T(8,128)} %param.7) | copy-start | bytes 196612
  0.9 0.8 %copy-start.3 = (bf16[128,2,64]{0,2,1:T(8,128)(2,1)S(1)}, bf16[128,2,64]{0,2,1:T(8,128)(2,1)}, u32[]{:S(2)}) copy-start(bf16[128,2,64]{0,2,1:T(8,128)(2,1)} %param.6) | copy-start | bytes 98308
  1.7 0.7 %copy-start.4 = (s32[128,2]{0,1:T(2,128)S(1)}, s32[128,2]{0,1:T(2,128)}, u32[]{:S(2)}) copy-start(s32[128,2]{0,1:T(2,128)} %param.9) | copy-start | bytes 3076
  2.4 0.7 %copy-start.5 = (s32[128,1]{0,1:T(1,128)S(1)}, s32[128,1]{0,1:T(1,128)}, u32[]{:S(2)}) copy-start(s32[128,1]{0,1:T(1,128)} %param.8) | copy-start | bytes 1540
  34.7 1.2 %copy-start.1 = (bf16[512,1024]{1,0:T(8,128)(2,1)S(1)}, bf16[512,1024]{1,0:T(8,128)(2,1)}, u32[]{:S(2)}) copy-start(bf16[512,1024]{1,0:T(8,128)(2,1)} %constant.2.clone.row_ref) | copy-start | bytes 3145732

commit v3 on v2

--- a/solution.py
+++ b/solution.py
@@ -18,13 +18,14 @@
 KINDS = 4
 ROWS = CAP * KINDS
 BLOCK = 64
-CHUNK = 32
+CHUNK = 16
 CHUNKS = GRID // CHUNK
-UNROLL = 4
+UNROLL = 8
 BF16 = jnp.bfloat16
 F32 = jnp.float32
 MESH = pl.DeviceIdType.MESH
 VMEM = pl.BlockSpec(memory_space=pltpu.VMEM)
+HBM = pl.BlockSpec(memory_space=pltpu.HBM)
 NT = (((1,), (1,)), ((), ()))
 
 
@@ -50,27 +51,43 @@
     return 1.0 - 2.0 * s * s, 2.0 * s * c
 
 
-def route_kernel(vis_ref, ang_ref, route_ref, off_ref, out_ref, send, recv, send_sem, recv_sem):
-    z, f = lax.axis_index("wa"), lax.axis_index("facet")
-    x, y, core = f >> 3, (f >> 1) & 3, f & 1
-    me = z * 32 + f
-
-    def peer(k):
-        def far_first(n):
-            return jnp.where(n == 0, 2, jnp.where(n == 3, 0, jnp.where(n == 1, 1, 3)))
-
-        z_to = (z + far_first(k >> 5)) & 3
-        x_to = (x + far_first((k >> 3) & 3)) & 3
-        y_to = (y + far_first((k >> 1) & 3)) & 3
-        return z_to, (x_to << 3) | (y_to << 1) | (core ^ (k & 1) ^ 1)
+def route_kernel(
+    vis_hbm, ang_hbm, route_hbm, off_hbm, out_ref, vis_ref, ang_ref, route_ref, off_ref, send, recv,
+    in_sems, send_sem, recv_sem,
+):
+    inputs = [
+        pltpu.make_async_copy(source, target, in_sems.at[n])
+        for n, (source, target) in enumerate(
+            ((route_hbm, route_ref), (off_hbm, off_ref), (ang_hbm, ang_ref), (vis_hbm, vis_ref))
+        )
+    ]
+    for copy in inputs:
+        copy.start()
+
+    me = lax.axis_index("wa") * 32 + lax.axis_index("facet")
+
+    def each_peer(act):
+        def early(i, carry):
+            for n in range(5):
+                act(me ^ (i * 5 + n) ^ 85)
+            return carry
+
+        def late(i, carry):
+            for n in range(6):
+                act(me ^ (i * 6 + n + 86) ^ 85)
+            return carry
+
+        lax.fori_loop(0, 17, early, 0)
+        lax.fori_loop(0, 7, late, 0)
 
     barrier = pltpu.get_barrier_semaphore()
-
-    def greet(k, carry):
-        pl.semaphore_signal(barrier, inc=1, device_id=peer(k), device_id_type=MESH)
-        return carry
-
-    lax.fori_loop(0, SUBS - 1, greet, 0)
+    each_peer(
+        lambda to: pl.semaphore_signal(
+            barrier, inc=1, device_id=(to >> 5, to & 31), device_id_type=MESH
+        )
+    )
+    for copy in inputs:
+        copy.wait()
 
     owner = route_ref[...]
     facet = owner & 31
@@ -112,15 +129,12 @@
 
     pl.semaphore_wait(barrier, SUBS - 1)
 
-    def post(k, carry):
-        z_to, f_to = peer(k)
-        pltpu.make_async_remote_copy(
-            src_ref=send.at[z_to * 32 + f_to], dst_ref=recv.at[me], send_sem=send_sem, recv_sem=recv_sem,
-            device_id=(z_to, f_to), device_id_type=MESH,
+    each_peer(
+        lambda to: pltpu.make_async_remote_copy(
+            src_ref=send.at[to], dst_ref=recv.at[me], send_sem=send_sem, recv_sem=recv_sem,
+            device_id=(to >> 5, to & 31), device_id_type=MESH,
         ).start()
-        return carry
-
-    lax.fori_loop(0, SUBS - 1, post, 0)
+    )
     recv[me] = send[me]
     others = pl.ds(0, SUBS - 1)
     pltpu.make_async_copy(send.at[others], recv.at[others], recv_sem).wait()
@@ -132,11 +146,16 @@
     return pl.pallas_call(
         route_kernel,
         out_shape=jax.ShapeDtypeStruct((SUBS, ROWS, 128), BF16),
-        in_specs=[VMEM] * 4,
+        in_specs=[HBM] * 4,
         out_specs=VMEM,
         scratch_shapes=[
+            pltpu.VMEM((2 * NVIS, SUBS), BF16),
+            pltpu.VMEM((2 * NVIS, SUBS), F32),
+            pltpu.VMEM((1, SUBS), jnp.int32),
+            pltpu.VMEM((2, SUBS), jnp.int32),
             pltpu.VMEM((SUBS, ROWS, 128), BF16),
             pltpu.VMEM((SUBS, ROWS, 128), BF16),
+            pltpu.SemaphoreType.DMA((4,)),
             pltpu.SemaphoreType.DMA,
             pltpu.SemaphoreType.DMA,
         ],
@@ -144,7 +163,7 @@
             collective_id=0, has_side_effects=True, vmem_limit_bytes=8 << 20
         ),
         name="route",
-    )(vis, ang, owners, off)
+    )(*[pltpu.with_memory_space_constraint(value, pltpu.HBM) for value in (vis, ang, owners, off)])
 
 
 def complex_mul(a, b):
@@ -152,9 +171,11 @@
 
 
 def grid_kernel(
-    recv_ref, grid_ref, wide, pos_v, pos_s, pos_sem, au_r, au_i, av_r, av_i, bu, bv, acc_a, acc_b, sub_a, sub_b
+    recv_ref, rows_hbm, grid_ref, rows_ref, wide, pos_v, pos_s, pos_sem, rows_sem, au_r, au_i, av_r, av_i, bu, bv, acc_a, acc_b, lefts, rights, subs
 ):
     slots = SUBS * CAP
+    rows_copy = pltpu.make_async_copy(rows_hbm, rows_ref, rows_sem)
+    rows_copy.start()
     wide[...] = recv_ref[...].astype(F32)
 
     lane8 = lax.broadcasted_iota(jnp.int32, (8, 128), 1)
@@ -169,14 +190,18 @@
     to_scalar = pltpu.make_async_copy(pos_v, pos_s, pos_sem)
     to_scalar.start()
 
-    acc_a[...] = jnp.zeros_like(acc_a)
-    acc_b[...] = jnp.zeros_like(acc_b)
-    sub_b[...] = jnp.zeros_like(sub_b)
+    lefts[...] = jnp.zeros_like(lefts)
+    rights[...] = jnp.zeros_like(rights)
+    subs[...] = jnp.zeros_like(subs)
 
     group = 16
     first = lax.broadcasted_iota(jnp.int32, (group, 128), 1) < 64
 
     def tables(g, carry):
+        clear = pl.ds(pl.multiple_of(g * SUB, SUB), SUB)
+        for tile in range(GRID // SUB + 1):
+            acc_a[tile, clear, :] = jnp.zeros((SUB, 128), F32)
+            acc_b[tile, clear, :] = jnp.zeros((SUB, 128), F32)
         for j in range(CAP):
             start = g * group
 
@@ -226,7 +251,7 @@
 
     lane_in = lax.broadcasted_iota(jnp.int32, (SUB, 128), 1) & 63
 
-    def form(slot):
+    def form(n, slot):
         base = pl.multiple_of(slot * 8, 8)
         ur, ui = au_r[pl.ds(base, 8), :], au_i[pl.ds(base, 8), :]
         vr, vi = av_r[pl.ds(base, 8), :], av_i[pl.ds(base, 8), :]
@@ -251,63 +276,87 @@
             if b < 3:
                 right_r[5 + b] = x - y
                 right_i[5 + b] = z + w
-        left = jnp.concatenate(left, axis=0).astype(BF16)
-        right = jnp.concatenate(right_r + right_i, axis=0).astype(BF16)
-        return lax.dot_general(left, right, NT, preferred_element_type=F32)
+        lefts[n] = jnp.concatenate(left, axis=0).astype(BF16)
+        rights[n] = jnp.concatenate(right_r + right_i, axis=0).astype(BF16)
+
+    nought = jnp.zeros((SUB, 128), BF16)
+
+    def multiply(n):
+        left = jnp.concatenate(
+            [jnp.concatenate([lefts[n], nought], axis=1), jnp.concatenate([nought, lefts[n + 1]], axis=1)],
+            axis=0,
+        )
+        right = jnp.concatenate([rights[n], rights[n + 1]], axis=1)
+        subs[n // 2] = lax.dot_general(left, right, NT, preferred_element_type=F32).astype(BF16)
 
     def place(slot, sub, acc):
         packed = pos_s[slot >> 7, 0, slot & (SUBS - 1)]
         off_u, off_v = packed >> 9, packed & 511
         tile, shift = off_v >> 6, off_v & 63
-        turned = pltpu.roll(sub, shift, 1)
         rows = pl.ds(off_u, SUB)
         here, there = acc.at[tile, rows, :], acc.at[tile + 1, rows, :]
-        near = here[...] + turned
-        far = there[...] + pltpu.roll(turned, 64, 1)
+        near = here[...] + pltpu.roll(sub, shift, 1).astype(F32)
+        far = there[...] + pltpu.roll(sub, shift + 64, 1).astype(F32)
         pltpu.store(here, near, mask=lane_in >= shift)
         pltpu.store(there, far, mask=lane_in < shift)
 
+    def place_all(start):
+        for n in range(UNROLL):
+            sub = subs[n // 2, pl.ds(n % 2 * SUB, SUB), :]
+            place(start + n, sub, (acc_a, acc_b)[n % 2])
+
+    def multiply_all():
+        for n in range(0, UNROLL, 2):
+            multiply(n)
+
     def work(i, carry):
-        now = i * (2 * UNROLL)
-        before = jnp.maximum(now - UNROLL, 0)
+        place_all(jnp.maximum(i - 2, 0) * UNROLL)
+        multiply_all()
         for n in range(UNROLL):
-            sub_a[n] = form(now + n)
-        for n in range(UNROLL):
-            place(before + n, sub_b[n], (acc_a, acc_b)[n % 2])
-        for n in range(UNROLL):
-            sub_b[n] = form(now + UNROLL + n)
-        for n in range(UNROLL):
-            place(now + n, sub_a[n], (acc_a, acc_b)[n % 2])
+            form(n, i * UNROLL + n)
         return carry
 
-    lax.fori_loop(0, slots // (2 * UNROLL), work, 0)
-    for n in range(UNROLL):
-        place(slots - UNROLL + n, sub_b[n], (acc_a, acc_b)[n % 2])
-
-    for tile in range(GRID // SUB):
-        grid_ref[:, pl.ds(tile * 128, 128)] = (acc_a[tile] + acc_b[tile]).astype(BF16)
-
-
-def grid_owner(recv):
+    lax.fori_loop(0, slots // UNROLL, work, 0)
+    place_all(slots - 2 * UNROLL)
+    multiply_all()
+    place_all(slots - UNROLL)
+
+    def finish(g, carry):
+        rows = pl.ds(pl.multiple_of(g * SUB, SUB), SUB)
+        for tile in range(GRID // SUB):
+            grid_ref[rows, pl.ds(tile * 128, 128)] = (acc_a[tile, rows, :] + acc_b[tile, rows, :]).astype(BF16)
+        return carry
+
+    lax.fori_loop(0, GRID // SUB, finish, 0)
+    rows_copy.wait()
+
+
+def grid_owner(recv, row_table):
     slots = SUBS * CAP
+    band = jax.ShapeDtypeStruct((GRID, 2 * GRID), BF16)
     return pl.pallas_call(
         grid_kernel,
-        out_shape=jax.ShapeDtypeStruct((GRID, 2 * GRID), BF16),
-        in_specs=[VMEM],
-        out_specs=VMEM,
+        out_shape=(band, band),
+        in_specs=[VMEM, HBM],
+        out_specs=(VMEM, VMEM),
         scratch_shapes=[
             pltpu.VMEM((SUBS * ROWS, 128), F32),
             pltpu.VMEM((CAP, 8, 128), jnp.int32),
             pltpu.SMEM((CAP, 8, 128), jnp.int32),
             pltpu.SemaphoreType.DMA,
+            pltpu.SemaphoreType.DMA,
         ]
         + [pltpu.VMEM((slots * 8, 128), F32)] * 4
         + [pltpu.VMEM((8, slots, 128), F32)] * 2
         + [pltpu.VMEM((GRID // SUB + 1, GRID, 128), F32)] * 2
-        + [pltpu.VMEM((UNROLL, SUB, 128), F32)] * 2,
+        + [
+            pltpu.VMEM((UNROLL, SUB, 128), BF16),
+            pltpu.VMEM((UNROLL, 2 * SUB, 128), BF16),
+            pltpu.VMEM((UNROLL // 2, 2 * SUB, 128), BF16),
+        ],
         compiler_params=pltpu.CompilerParams(vmem_limit_bytes=22 << 20),
         name="grid",
-    )(recv)
+    )(recv, pltpu.with_memory_space_constraint(row_table, pltpu.HBM))
 
 
 def chain_kernel(
@@ -512,8 +561,8 @@
     vis = visibilities.transpose(1, 2, 0).reshape(2 * NVIS, SUBS)
     ang = uv_angles.transpose(1, 2, 0).reshape(2 * NVIS, SUBS)
     recv = route(vis, ang, routes.reshape(1, SUBS), offsets.T)
-    grid = grid_owner(recv.reshape(SUBS * ROWS, 128))
-    result = chain(grid, jnp.asarray(dft_rows()), pixel_phase[0])
+    grid, row_table = grid_owner(recv.reshape(SUBS * ROWS, 128), jnp.asarray(dft_rows()))
+    result = chain(grid, row_table, pixel_phase[0])
     return result.astype(F32).reshape(1, 1, GRID, 2 * GRID)
 
 

time: 60.4 us -> 52.4 us (0.87)
  local copies, waits for them, and re-layouts: 4.24 us -> 0.01 us
  Pallas kernels: 54.4 us -> 50.7 us
    unnamed x12 -> x2, local copies, waits for them, and re-layouts: 4.24 us -> 0.01 us
    pallas_call x1, Pallas kernels: 14.8 us -> 11.1 us  [grid_owner(): pl.pallas_call(grid_kernel, out_shape=(band, band), in_specs=[VMEM, HBM],...]
    pallas_call x1, Pallas kernels: 22.7 us -> 23.5 us  [chain(): pl.pallas_call(chain_kernel, out_shape=jax.ShapeDtypeStruct(band, BF16),...]
    pallas_call x1, Pallas kernels: 16.9 us -> 16.1 us  [route(): pl.pallas_call(route_kernel, out_shape=jax.ShapeDtypeStruct((SUBS, ROWS,...]
where the time goes in v3:
time: 52.4 us; the launch traced here: 52.3 us
  Pallas kernels  50.7 us (97%)
  other arithmetic  1.57 us (3%)
    pallas_call x1, Pallas kernels, chain(): pl.pallas_call(chain_kernel, out_shape=jax.ShapeDtypeStruct(band, BF16),...  23.5 us
    pallas_call x1, Pallas kernels, route(): pl.pallas_call(route_kernel, out_shape=jax.ShapeDtypeStruct((SUBS, ROWS,...  16.1 us
    pallas_call x1, Pallas kernels, grid_owner(): pl.pallas_call(grid_kernel, out_shape=(band, band), in_specs=[VMEM, HBM],...  11.1 us
    reshape x1, other arithmetic, on_device(): return result.astype(F32).reshape(1, 1, GRID, 2 * GRID)  1.57 us

profile of v3, /device:TPU:1, one launch (start us, length us, event | category | flops | bytes accessed | tf_op | source)
XLA Modules:
  0.0 52.3 jit_solution(1275309098566912311)
XLA Ops:
  0.0 0.0 copy-start
  0.0 16.1 %route.1 = bf16[128,8,128]{2,1,0:T(8,128)(2,1)S(1)} custom-call(bf16[128,128]{1,0:T(8,128)(2,1)} %bitcast.16, f32[128,128]{1,0:T(8,128)} %bitcast.15, s32[1,128]{1,0:T(1,128)} %bitcast.18, s32[2,128]{1,0:T(2,128)} %bitcast.17), custom_call_target="tpu_custom_call" | custom-call | tf_op jit(solution)/shard_map/route/pallas_call | solution.py:146
  16.1 11.1 %grid.1 = (bf16[512,1024]{1,0:T(8,128)(2,1)S(1)}, bf16[512,1024]{1,0:T(8,128)(2,1)S(1)}) custom-call(bf16[1024,128]{1,0:T(8,128)(2,1)S(1)} %bitcast.13, bf16[512,1024]{1,0:T(8,128)(2,1)} %constant.2.clone.rows_hbm), custom_call_target="tpu_custom_call" | custom-call | tf_op jit(solution)/shard_map/grid/pallas_call | solution.py:337
  27.2 0.0 copy-done
  27.2 23.5 %chain.1 = bf16[512,1024]{1,0:T(8,128)(2,1)S(1)} custom-call(bf16[512,1024]{1,0:T(8,128)(2,1)S(1)} %get-tuple-element.7.grid_ref, bf16[512,1024]{1,0:T(8,128)(2,1)S(1)} %get-tuple-element.8.row_ref, f32[512,512]{1,0:T(8,128)S(1)} %bitcast.14), custom_call_target="tpu_custom_call" | custom-call | tf_op jit(solution)/shard_map/chain/pallas_call | solution.py:529
  50.7 1.6 %bitcast_convert_fusion = f32[1,1,512,1024]{3,2,1,0:T(8,128)} fusion(bf16[512,1024]{1,0:T(8,128)(2,1)S(1)} %chain.1), kind=kLoop, calls=%fused_computation | loop fusion | flops 524288 | bytes 3145728 | tf_op jit(solution)/shard_map/reshape | solution.py:566
Async XLA Ops:
  0.0 27.2 %copy-start = (f32[1,512,512]{2,1,0:T(8,128)S(1)}, f32[1,512,512]{2,1,0:T(8,128)}, u32[]{:S(2)}) copy-start(f32[1,512,512]{2,1,0:T(8,128)} %param.10) | copy-start | bytes 3145732

commit v4 on v3

--- a/solution.py
+++ b/solution.py
@@ -18,7 +18,9 @@
 KINDS = 4
 ROWS = CAP * KINDS
 BLOCK = 64
-CHUNK = 16
+CHUNK = 32
+BLOCKS = GRID // BLOCK
+PARTS = BLOCK // CHUNK
 CHUNKS = GRID // CHUNK
 UNROLL = 8
 BF16 = jnp.bfloat16
@@ -52,8 +54,8 @@
 
 
 def route_kernel(
-    vis_hbm, ang_hbm, route_hbm, off_hbm, out_ref, vis_ref, ang_ref, route_ref, off_ref, send, recv,
-    in_sems, send_sem, recv_sem,
+    vis_hbm, ang_hbm, route_hbm, off_hbm, phase_hbm, out_ref, p_re, p_im, vis_ref, ang_ref, route_ref, off_ref, phase,
+    send, recv, in_sems, send_sem, recv_sem, p_sems,
 ):
     inputs = [
         pltpu.make_async_copy(source, target, in_sems.at[n])
@@ -64,7 +66,24 @@
     for copy in inputs:
         copy.start()
 
-    me = lax.axis_index("wa") * 32 + lax.axis_index("facet")
+    z, f = lax.axis_index("wa"), lax.axis_index("facet")
+    me = z * 32 + f
+
+    low, core = z < 2, f & 1
+    takes = (low & (core == 1)) | (jnp.logical_not(low) & (core == 0))
+
+    def phase_own():
+        return pltpu.make_async_copy(phase_hbm, phase, p_sems.at[2])
+
+    def phase_out():
+        return pltpu.make_async_remote_copy(
+            src_ref=phase_hbm, dst_ref=phase, send_sem=p_sems.at[0], recv_sem=p_sems.at[1],
+            device_id=(z, f ^ 1), device_id_type=MESH,
+        )
+
+    @pl.when(jnp.logical_not(takes))
+    def _():
+        phase_own().start()
 
     def each_peer(act):
         def early(i, carry):
@@ -129,6 +148,10 @@
 
     pl.semaphore_wait(barrier, SUBS - 1)
 
+    @pl.when(jnp.logical_not(takes))
+    def _():
+        phase_out().start()
+
     each_peer(
         lambda to: pltpu.make_async_remote_copy(
             src_ref=send.at[to], dst_ref=recv.at[me], send_sem=send_sem, recv_sem=recv_sem,
@@ -136,34 +159,59 @@
         ).start()
     )
     recv[me] = send[me]
+
+    @pl.when(takes)
+    def _():
+        phase_out().wait_recv()
+
+    @pl.when(jnp.logical_not(takes))
+    def _():
+        phase_own().wait()
+
+    def angles(i, carry):
+        rows = pl.ds(pl.multiple_of(i * BLOCK, BLOCK), BLOCK)
+        c, s = sincos(phase[rows, :])
+        p_re[rows, :] = c
+        p_im[rows, :] = s
+        return carry
+
+    lax.fori_loop(0, BLOCKS, angles, 0)
+
     others = pl.ds(0, SUBS - 1)
     pltpu.make_async_copy(send.at[others], recv.at[others], recv_sem).wait()
     out_ref[...] = recv[...]
     pltpu.make_async_copy(send.at[others], recv.at[others], send_sem).wait()
 
-
-def route(vis, ang, owners, off):
+    @pl.when(jnp.logical_not(takes))
+    def _():
+        phase_out().wait_send()
+
+
+def route(vis, ang, owners, off, phase):
+    pixels = jax.ShapeDtypeStruct((GRID, GRID), F32)
     return pl.pallas_call(
         route_kernel,
-        out_shape=jax.ShapeDtypeStruct((SUBS, ROWS, 128), BF16),
-        in_specs=[HBM] * 4,
-        out_specs=VMEM,
+        out_shape=(jax.ShapeDtypeStruct((SUBS, ROWS, 128), BF16), pixels, pixels),
+        in_specs=[HBM] * 5,
+        out_specs=(VMEM, VMEM, VMEM),
         scratch_shapes=[
             pltpu.VMEM((2 * NVIS, SUBS), BF16),
             pltpu.VMEM((2 * NVIS, SUBS), F32),
             pltpu.VMEM((1, SUBS), jnp.int32),
             pltpu.VMEM((2, SUBS), jnp.int32),
+            pltpu.VMEM((GRID, GRID), F32),
             pltpu.VMEM((SUBS, ROWS, 128), BF16),
             pltpu.VMEM((SUBS, ROWS, 128), BF16),
             pltpu.SemaphoreType.DMA((4,)),
             pltpu.SemaphoreType.DMA,
             pltpu.SemaphoreType.DMA,
+            pltpu.SemaphoreType.DMA((3,)),
         ],
         compiler_params=pltpu.CompilerParams(
-            collective_id=0, has_side_effects=True, vmem_limit_bytes=8 << 20
+            collective_id=0, has_side_effects=True, vmem_limit_bytes=10 << 20
         ),
         name="route",
-    )(*[pltpu.with_memory_space_constraint(value, pltpu.HBM) for value in (vis, ang, owners, off)])
+    )(*[pltpu.with_memory_space_constraint(value, pltpu.HBM) for value in (vis, ang, owners, off, phase)])
 
 
 def complex_mul(a, b):
@@ -360,8 +408,8 @@
 
 
 def chain_kernel(
-    grid_ref, row_ref, phase_ref, out_ref, col, phase, p_re, p_im, image, from_h, from_s, mine,
-    h_recv, s_recv, h_send, s_send, p_sems,
+    grid_ref, row_ref, p_re, p_im, out_ref, col, image, from_h, from_s, from_x, mine, other,
+    h_recv, s_recv, x_recv, h_send, s_send, x_send,
 ):
     z, f = lax.axis_index("wa"), lax.axis_index("facet")
     core = f & 1
@@ -381,50 +429,54 @@
     for step in range(1, 8):
         pl.semaphore_signal(barrier, inc=1, device_id=at((seat + step) & 7), device_id_type=MESH)
 
-    gives = is_seat(0, 2, 5)
-    takes = is_seat(1, 3, 4)
-    keeps = is_seat(2, 5, 7)
-
-    def phase_out():
-        return pltpu.make_async_remote_copy(
-            src_ref=phase_ref, dst_ref=phase, send_sem=p_sems.at[0], recv_sem=p_sems.at[1],
-            device_id=at(seat ^ 1), device_id_type=MESH,
-        )
-
-    def phase_own():
-        return pltpu.make_async_copy(phase_ref, phase, p_sems.at[2])
-
-    @pl.when(keeps)
-    def _():
-        phase_own().start()
-
     for tile in range(GRID // SUB):
         rows = row_ref[pl.ds(tile * SUB, SUB), :]
         col[pl.ds(tile * 128, SUB), :] = rows
         col[pl.ds(tile * 128 + SUB, SUB), pl.ds(0, GRID)] = -rows[:, GRID:]
         col[pl.ds(tile * 128 + SUB, SUB), pl.ds(GRID, GRID)] = rows[:, :GRID]
 
+    real = lax.broadcasted_iota(jnp.int32, (BLOCK, 2 * GRID), 1) & 127 < 64
+
+    def block_rows(i):
+        return pl.ds(pl.multiple_of(i * BLOCK, BLOCK), BLOCK)
+
+    def chunk_rows(i):
+        return pl.ds(pl.multiple_of(i * CHUNK, CHUNK), CHUNK)
+
+    def transform(i):
+        rows = block_rows(i)
+        both = jnp.concatenate([row_ref[rows, pl.ds(0, GRID)], row_ref[rows, pl.ds(GRID, GRID)]], axis=0)
+        parts = jnp.dot(both, grid_ref[...], preferred_element_type=F32)
+        turned = jnp.concatenate(
+            [pltpu.roll(parts[BLOCK:, t * 128 : (t + 1) * 128], 64, 1) for t in range(GRID // SUB)], axis=1
+        )
+        half = parts[:BLOCK] + jnp.where(real, -turned, turned)
+        image[rows, :] = jnp.dot(half.astype(BF16), col[...], preferred_element_type=F32)
+
+    transform(0)
     pl.semaphore_wait(barrier, 7)
-
-    @pl.when(gives)
-    def _():
-        phase_out().start()
 
     to_h = jnp.where(seat == 0, 2, jnp.where(seat == 2, 3, jnp.where(seat == 3, 1,
            jnp.where(seat == 6, 4, jnp.where(seat == 4, 5, 7)))))
     to_s = jnp.where(seat == 1, 6, jnp.where(seat == 3, 4, jnp.where(seat == 4, 3, 1)))
     sends_h = is_seat(0, 2, 3, 4, 5, 6)
     takes_h = is_seat(1, 2, 3, 4, 5, 7)
+    sends_x = is_seat(0, 2)
     away = is_seat(1, 3, 4, 6)
-
-    def chunk_rows(i):
-        return pl.ds(pl.multiple_of(i * CHUNK, CHUNK), CHUNK)
-
-    def copy_h(i):
+    lag = jnp.where(is_seat(2, 4), 1, 3)
+
+    def copy_h(i, source=mine):
         rows = chunk_rows(i)
         return pltpu.make_async_remote_copy(
-            src_ref=mine.at[rows], dst_ref=from_h.at[rows], send_sem=h_send.at[i], recv_sem=h_recv.at[i],
+            src_ref=source.at[rows], dst_ref=from_h.at[rows], send_sem=h_send.at[i], recv_sem=h_recv.at[i],
             device_id=at(to_h), device_id_type=MESH,
+        )
+
+    def copy_x(i, source=mine):
+        rows = chunk_rows(i)
+        return pltpu.make_async_remote_copy(
+            src_ref=source.at[rows], dst_ref=from_x.at[rows], send_sem=x_send.at[i], recv_sem=x_recv.at[i],
+            device_id=at(seat | 1), device_id_type=MESH,
         )
 
     def copy_s(i):
@@ -434,68 +486,95 @@
             device_id=at(to_s), device_id_type=MESH,
         )
 
-    real = lax.broadcasted_iota(jnp.int32, (BLOCK, 2 * GRID), 1) & 127 < 64
-
-    def work(i, carry):
-        rows = pl.ds(pl.multiple_of(i * BLOCK, BLOCK), BLOCK)
-        both = jnp.concatenate([row_ref[rows, pl.ds(0, GRID)], row_ref[rows, pl.ds(GRID, GRID)]], axis=0)
-        parts = jnp.dot(both, grid_ref[...], preferred_element_type=F32)
-        turned = jnp.concatenate(
-            [pltpu.roll(parts[BLOCK:, t * 128 : (t + 1) * 128], 64, 1) for t in range(GRID // SUB)], axis=1
-        )
-        half = parts[:BLOCK] + jnp.where(real, -turned, turned)
-        image[...] = jnp.dot(half.astype(BF16), col[...], preferred_element_type=F32)
-
-        @pl.when(takes_h)
+    def turn(rows, re, im):
+        c, s = p_re[rows, :], p_im[rows, :]
+        return c * re - s * im, c * im + s * re
+
+    def halves(ref, rows):
+        return ref[rows, pl.ds(0, GRID)].astype(F32), ref[rows, pl.ds(GRID, GRID)].astype(F32)
+
+    def keep(ref, rows, re, im):
+        ref[rows, pl.ds(0, GRID)] = re.astype(BF16)
+        ref[rows, pl.ds(GRID, GRID)] = im.astype(BF16)
+
+    def plus(rows, ref, pair_in):
+        re, im = halves(ref, rows)
+        return pair_in[0] + re, pair_in[1] + im
+
+    def work(t, carry):
+        @pl.when(t < BLOCKS)
         def _():
-            @pl.when(i == 0)
+            @pl.when(is_seat(0, 6))
             def _():
-                @pl.when(takes)
+                for part in range(PARTS):
+                    i = t * PARTS + part
+                    mine[chunk_rows(i), :] = image[chunk_rows(i), :].astype(BF16)
+                    copy_h(i).start()
+
+                    @pl.when(seat == 0)
+                    def _():
+                        copy_x(i).start()
+                        out_ref[chunk_rows(i), :] = mine[chunk_rows(i), :]
+
+                    @pl.when(seat == 6)
+                    def _():
+                        copy_s(i).start()
+
+            @pl.when(seat == 2)
+            def _():
+                for part in range(PARTS):
+                    i = t * PARTS + part
+                    other[chunk_rows(i), :] = image[chunk_rows(i), :].astype(BF16)
+                    copy_x(i, other).start()
+
+            @pl.when(t < BLOCKS - 1)
+            def _():
+                transform(t + 1)
+
+            @pl.when(seat == 3)
+            def _():
+                for part in range(PARTS):
+                    i = t * PARTS + part
+                    rows = chunk_rows(i)
+                    copy_x(i).wait_recv()
+                    keep(other, rows, *plus(rows, image, turn(rows, *halves(from_x, rows))))
+                    copy_h(i, other).start()
+
+        block = t - lag
+
+        @pl.when(takes_h & (block >= 0) & (block < BLOCKS))
+        def _():
+            for part in range(PARTS):
+                i = block * PARTS + part
+                rows = chunk_rows(i)
+
+                @pl.when(seat == 1)
                 def _():
-                    phase_out().wait_recv()
-
-                @pl.when(keeps)
+                    copy_x(i).wait_recv()
+                    twice = turn(rows, *turn(rows, *halves(from_x, rows)))
+                    copy_h(i).wait_recv()
+                    keep(mine, rows, *plus(rows, image, turn(rows, *plus(rows, from_h, twice))))
+
+                @pl.when(seat != 1)
                 def _():
-                    phase_own().wait()
-
-            c, s = sincos(phase[rows, :])
-            p_re[...] = c
-            p_im[...] = s
-
-        for part in range(BLOCK // CHUNK):
-            chunk = i * (BLOCK // CHUNK) + part
-            at_rows = chunk_rows(chunk)
-            local = pl.ds(part * CHUNK, CHUNK)
-
-            @pl.when(takes_h)
-            def _():
-                copy_h(chunk).wait_recv()
-                f_re = from_h[at_rows, pl.ds(0, GRID)].astype(F32)
-                f_im = from_h[at_rows, pl.ds(GRID, GRID)].astype(F32)
-                c, s = p_re[local, :], p_im[local, :]
-                im_re, im_im = image[local, pl.ds(0, GRID)], image[local, pl.ds(GRID, GRID)]
-                mine[at_rows, pl.ds(0, GRID)] = (c * f_re - s * f_im + im_re).astype(BF16)
-                mine[at_rows, pl.ds(GRID, GRID)] = (c * f_im + s * f_re + im_im).astype(BF16)
-
-            @pl.when(jnp.logical_not(takes_h))
-            def _():
-                mine[at_rows, :] = image[local, :].astype(BF16)
-
-            @pl.when(sends_h)
-            def _():
-                copy_h(chunk).start()
-
-            @pl.when(away)
-            def _():
-                copy_s(chunk).start()
-
-            @pl.when(jnp.logical_not(away))
-            def _():
-                out_ref[at_rows, :] = mine[at_rows, :]
+                    copy_h(i).wait_recv()
+                    keep(mine, rows, *plus(rows, image, turn(rows, *halves(from_h, rows))))
+
+                @pl.when(is_seat(2, 4, 5))
+                def _():
+                    copy_h(i).start()
+
+                @pl.when(is_seat(1, 3, 4))
+                def _():
+                    copy_s(i).start()
+
+                @pl.when(is_seat(2, 5, 7))
+                def _():
+                    out_ref[rows, :] = mine[rows, :]
 
         return carry
 
-    lax.fori_loop(0, GRID // BLOCK, work, 0)
+    lax.fori_loop(0, BLOCKS + 3, work, 0)
 
     @pl.when(away)
     def _():
@@ -506,15 +585,15 @@
 
         lax.fori_loop(0, CHUNKS, finish, 0)
 
-    @pl.when(gives)
-    def _():
-        phase_out().wait_send()
-
     def drain(i, carry):
         @pl.when(sends_h)
         def _():
             copy_h(i).wait_send()
 
+        @pl.when(sends_x)
+        def _():
+            copy_x(i).wait_send()
+
         @pl.when(away)
         def _():
             copy_s(i).wait_send()
@@ -524,30 +603,24 @@
     lax.fori_loop(0, CHUNKS, drain, 0)
 
 
-def chain(grid, row_table, phase):
+def chain(grid, row_table, p_re, p_im):
     band = (GRID, 2 * GRID)
     return pl.pallas_call(
         chain_kernel,
         out_shape=jax.ShapeDtypeStruct(band, BF16),
-        in_specs=[VMEM, VMEM, pl.BlockSpec(memory_space=pl.ANY)],
+        in_specs=[VMEM] * 4,
         out_specs=VMEM,
         scratch_shapes=[
             pltpu.VMEM((2 * GRID, 2 * GRID), BF16),
-            pltpu.VMEM((GRID, GRID), F32),
-            pltpu.VMEM((BLOCK, GRID), F32),
-            pltpu.VMEM((BLOCK, GRID), F32),
-            pltpu.VMEM((BLOCK, 2 * GRID), F32),
-            pltpu.VMEM(band, BF16),
-            pltpu.VMEM(band, BF16),
-            pltpu.VMEM(band, BF16),
+            pltpu.VMEM(band, F32),
         ]
-        + [pltpu.SemaphoreType.DMA((CHUNKS,))] * 4
-        + [pltpu.SemaphoreType.DMA((3,))],
+        + [pltpu.VMEM(band, BF16)] * 5
+        + [pltpu.SemaphoreType.DMA((CHUNKS,))] * 6,
         compiler_params=pltpu.CompilerParams(
-            collective_id=1, has_side_effects=True, vmem_limit_bytes=18 << 20
+            collective_id=1, has_side_effects=True, vmem_limit_bytes=24 << 20
         ),
         name="chain",
-    )(grid, row_table, phase)
+    )(grid, row_table, p_re, p_im)
 
 
 def dft_rows():
@@ -560,9 +633,9 @@
 def on_device(visibilities, uv_angles, routes, offsets, pixel_phase):
     vis = visibilities.transpose(1, 2, 0).reshape(2 * NVIS, SUBS)
     ang = uv_angles.transpose(1, 2, 0).reshape(2 * NVIS, SUBS)
-    recv = route(vis, ang, routes.reshape(1, SUBS), offsets.T)
+    recv, p_re, p_im = route(vis, ang, routes.reshape(1, SUBS), offsets.T, pixel_phase[0])
     grid, row_table = grid_owner(recv.reshape(SUBS * ROWS, 128), jnp.asarray(dft_rows()))
-    result = chain(grid, row_table, pixel_phase[0])
+    result = chain(grid, row_table, p_re, p_im)
     return result.astype(F32).reshape(1, 1, GRID, 2 * GRID)
 
 

time: 52.4 us -> 49.5 us (0.945)
  Pallas kernels: 50.7 us -> 47.3 us
    pallas_call x1, Pallas kernels: 23.5 us -> 20.1 us  [chain(): pl.pallas_call(chain_kernel, out_shape=jax.ShapeDtypeStruct(band, BF16),...]
where the time goes in v4:
time: 49.5 us; the launch traced here: 48.9 us
  Pallas kernels  47.3 us (96%)
  other arithmetic  1.57 us (3%)
    pallas_call x1, Pallas kernels, chain(): pl.pallas_call(chain_kernel, out_shape=jax.ShapeDtypeStruct(band, BF16),...  20.1 us
    pallas_call x1, Pallas kernels, route(): pl.pallas_call(route_kernel, out_shape=(jax.ShapeDtypeStruct((SUBS, ROWS,...  16 us
    pallas_call x1, Pallas kernels, grid_owner(): pl.pallas_call(grid_kernel, out_shape=(band, band), in_specs=[VMEM, HBM],...  11.1 us
    reshape x1, other arithmetic, on_device(): return result.astype(F32).reshape(1, 1, GRID, 2 * GRID)  1.57 us

profile of v4, /device:TPU:1, one launch (start us, length us, event | category | flops | bytes accessed | tf_op | source)
XLA Modules:
  0.0 48.9 jit_solution(14368479649941943732)
XLA Ops:
  0.0 16.0 %route.1 = (bf16[128,8,128]{2,1,0:T(8,128)(2,1)S(1)}, f32[512,512]{1,0:T(8,128)S(1)}, f32[512,512]{1,0:T(8,128)S(1)}) custom-call(bf16[128,128]{1,0:T(8,128)(2,1)} %bitcast.16, f32[128,128]{1,0:T(8,128)} %bitcast.15, s32[1,128]{1,0:T(1,128)} %bitcast.18, s32[2,128]{1,0:T(2,128)} %bitcast.17, f32[512,512]{1,0:T(8,128)} %bitcast.14), custom_call_target="tpu_custom_call" | custom-call | tf_op jit(solution)/shard_map/route/pallas_call | solution.py:192
  16.1 11.1 %grid.1 = (bf16[512,1024]{1,0:T(8,128)(2,1)S(1)}, bf16[512,1024]{1,0:T(8,128)(2,1)S(1)}) custom-call(bf16[1024,128]{1,0:T(8,128)(2,1)S(1)} %bitcast.13, bf16[512,1024]{1,0:T(8,128)(2,1)} %constant.2.clone.rows_hbm), custom_call_target="tpu_custom_call" | custom-call | tf_op jit(solution)/shard_map/grid/pallas_call | solution.py:385
  27.2 20.1 %chain.1 = bf16[512,1024]{1,0:T(8,128)(2,1)S(1)} custom-call(bf16[512,1024]{1,0:T(8,128)(2,1)S(1)} %get-tuple-element.11.grid_ref, bf16[512,1024]{1,0:T(8,128)(2,1)S(1)} %get-tuple-element.12.row_ref, f32[512,512]{1,0:T(8,128)S(1)} %get-tuple-element.13.p_re, f32[512,512]{1,0:T(8,128)S(1)} %get-tuple-element.14.p_im), custom_call_target="tpu_custom_call" | custom-call | tf_op jit(solution)/shard_map/chain/pallas_call | solution.py:608
  47.3 1.6 %bitcast_convert_fusion = f32[1,1,512,1024]{3,2,1,0:T(8,128)} fusion(bf16[512,1024]{1,0:T(8,128)(2,1)S(1)} %chain.1), kind=kLoop, calls=%fused_computation | loop fusion | flops 524288 | bytes 3145728 | tf_op jit(solution)/shard_map/reshape | solution.py:639

commit v5 on v4

--- a/solution.py
+++ b/solution.py
@@ -22,7 +22,7 @@
 BLOCKS = GRID // BLOCK
 PARTS = BLOCK // CHUNK
 CHUNKS = GRID // CHUNK
-UNROLL = 8
+UNROLL = 32
 BF16 = jnp.bfloat16
 F32 = jnp.float32
 MESH = pl.DeviceIdType.MESH

time: 49.5 us -> 47.6 us (0.962)
  Pallas kernels: 47.3 us -> 45.4 us
    pallas_call x1, Pallas kernels: 11.1 us -> 9.22 us  [grid_owner(): pl.pallas_call(grid_kernel, out_shape=(band, band), in_specs=[VMEM, HBM],...]
where the time goes in v5:
time: 47.6 us; the launch traced here: 47 us
  Pallas kernels  45.4 us (95%)
  other arithmetic  1.57 us (3%)
    pallas_call x1, Pallas kernels, chain(): pl.pallas_call(chain_kernel, out_shape=jax.ShapeDtypeStruct(band, BF16),...  20.2 us
    pallas_call x1, Pallas kernels, route(): pl.pallas_call(route_kernel, out_shape=(jax.ShapeDtypeStruct((SUBS, ROWS,...  16 us
    pallas_call x1, Pallas kernels, grid_owner(): pl.pallas_call(grid_kernel, out_shape=(band, band), in_specs=[VMEM, HBM],...  9.22 us
    reshape x1, other arithmetic, on_device(): return result.astype(F32).reshape(1, 1, GRID, 2 * GRID)  1.57 us

profile of v5, /device:TPU:1, one launch (start us, length us, event | category | flops | bytes accessed | tf_op | source)
XLA Modules:
  0.0 47.0 jit_solution(13203551579782469455)
XLA Ops:
  0.0 16.0 %route.1 = (bf16[128,8,128]{2,1,0:T(8,128)(2,1)S(1)}, f32[512,512]{1,0:T(8,128)S(1)}, f32[512,512]{1,0:T(8,128)S(1)}) custom-call(bf16[128,128]{1,0:T(8,128)(2,1)} %bitcast.16, f32[128,128]{1,0:T(8,128)} %bitcast.15, s32[1,128]{1,0:T(1,128)} %bitcast.18, s32[2,128]{1,0:T(2,128)} %bitcast.17, f32[512,512]{1,0:T(8,128)} %bitcast.14), custom_call_target="tpu_custom_call" | custom-call | tf_op jit(solution)/shard_map/route/pallas_call | solution.py:192
  16.1 9.2 %grid.1 = (bf16[512,1024]{1,0:T(8,128)(2,1)S(1)}, bf16[512,1024]{1,0:T(8,128)(2,1)S(1)}) custom-call(bf16[1024,128]{1,0:T(8,128)(2,1)S(1)} %bitcast.13, bf16[512,1024]{1,0:T(8,128)(2,1)} %constant.2.clone.rows_hbm), custom_call_target="tpu_custom_call" | custom-call | tf_op jit(solution)/shard_map/grid/pallas_call | solution.py:385
  25.3 20.2 %chain.1 = bf16[512,1024]{1,0:T(8,128)(2,1)S(1)} custom-call(bf16[512,1024]{1,0:T(8,128)(2,1)S(1)} %get-tuple-element.11.grid_ref, bf16[512,1024]{1,0:T(8,128)(2,1)S(1)} %get-tuple-element.12.row_ref, f32[512,512]{1,0:T(8,128)S(1)} %get-tuple-element.13.p_re, f32[512,512]{1,0:T(8,128)S(1)} %get-tuple-element.14.p_im), custom_call_target="tpu_custom_call" | custom-call | tf_op jit(solution)/shard_map/chain/pallas_call | solution.py:608
  45.4 1.6 %bitcast_convert_fusion = f32[1,1,512,1024]{3,2,1,0:T(8,128)} fusion(bf16[512,1024]{1,0:T(8,128)(2,1)S(1)} %chain.1), kind=kLoop, calls=%fused_computation | loop fusion | flops 524288 | bytes 3145728 | tf_op jit(solution)/shard_map/reshape | solution.py:639

commit v6 on v5

--- a/solution.py
+++ b/solution.py
@@ -219,7 +219,7 @@
 
 
 def grid_kernel(
-    recv_ref, rows_hbm, grid_ref, rows_ref, wide, pos_v, pos_s, pos_sem, rows_sem, au_r, au_i, av_r, av_i, bu, bv, acc_a, acc_b, lefts, rights, subs
+    recv_ref, rows_hbm, grid_ref, rows_ref, wide, pos_v, pos_s, pos_sem, rows_sem, au_r, au_i, av_r, av_i, bu, bv, acc_a, acc_b, subs
 ):
     slots = SUBS * CAP
     rows_copy = pltpu.make_async_copy(rows_hbm, rows_ref, rows_sem)
@@ -238,8 +238,6 @@
     to_scalar = pltpu.make_async_copy(pos_v, pos_s, pos_sem)
     to_scalar.start()
 
-    lefts[...] = jnp.zeros_like(lefts)
-    rights[...] = jnp.zeros_like(rights)
     subs[...] = jnp.zeros_like(subs)
 
     group = 16
@@ -299,7 +297,7 @@
 
     lane_in = lax.broadcasted_iota(jnp.int32, (SUB, 128), 1) & 63
 
-    def form(n, slot):
+    def form(slot):
         base = pl.multiple_of(slot * 8, 8)
         ur, ui = au_r[pl.ds(base, 8), :], au_i[pl.ds(base, 8), :]
         vr, vi = av_r[pl.ds(base, 8), :], av_i[pl.ds(base, 8), :]
@@ -324,18 +322,18 @@
             if b < 3:
                 right_r[5 + b] = x - y
                 right_i[5 + b] = z + w
-        lefts[n] = jnp.concatenate(left, axis=0).astype(BF16)
-        rights[n] = jnp.concatenate(right_r + right_i, axis=0).astype(BF16)
+        return jnp.concatenate(left, axis=0).astype(BF16), jnp.concatenate(right_r + right_i, axis=0).astype(BF16)
 
     nought = jnp.zeros((SUB, 128), BF16)
 
-    def multiply(n):
+    def form_pair(slot):
+        left_0, right_0 = form(slot)
+        left_1, right_1 = form(slot + 1)
         left = jnp.concatenate(
-            [jnp.concatenate([lefts[n], nought], axis=1), jnp.concatenate([nought, lefts[n + 1]], axis=1)],
-            axis=0,
-        )
-        right = jnp.concatenate([rights[n], rights[n + 1]], axis=1)
-        subs[n // 2] = lax.dot_general(left, right, NT, preferred_element_type=F32).astype(BF16)
+            [jnp.concatenate([left_0, nought], axis=1), jnp.concatenate([nought, left_1], axis=1)], axis=0
+        )
+        right = jnp.concatenate([right_0, right_1], axis=1)
+        return lax.dot_general(left, right, NT, preferred_element_type=F32).astype(BF16)
 
     def place(slot, sub, acc):
         packed = pos_s[slot >> 7, 0, slot & (SUBS - 1)]
@@ -353,20 +351,13 @@
             sub = subs[n // 2, pl.ds(n % 2 * SUB, SUB), :]
             place(start + n, sub, (acc_a, acc_b)[n % 2])
 
-    def multiply_all():
+    def work(i, carry):
+        place_all(jnp.maximum(i - 1, 0) * UNROLL)
         for n in range(0, UNROLL, 2):
-            multiply(n)
-
-    def work(i, carry):
-        place_all(jnp.maximum(i - 2, 0) * UNROLL)
-        multiply_all()
-        for n in range(UNROLL):
-            form(n, i * UNROLL + n)
+            subs[n // 2] = form_pair(i * UNROLL + n)
         return carry
 
     lax.fori_loop(0, slots // UNROLL, work, 0)
-    place_all(slots - 2 * UNROLL)
-    multiply_all()
     place_all(slots - UNROLL)
 
     def finish(g, carry):
@@ -398,8 +389,6 @@
         + [pltpu.VMEM((8, slots, 128), F32)] * 2
         + [pltpu.VMEM((GRID // SUB + 1, GRID, 128), F32)] * 2
         + [
-            pltpu.VMEM((UNROLL, SUB, 128), BF16),
-            pltpu.VMEM((UNROLL, 2 * SUB, 128), BF16),
             pltpu.VMEM((UNROLL // 2, 2 * SUB, 128), BF16),
         ],
         compiler_params=pltpu.CompilerParams(vmem_limit_bytes=22 << 20),
@@ -409,7 +398,7 @@
 
 def chain_kernel(
     grid_ref, row_ref, p_re, p_im, out_ref, col, image, from_h, from_s, from_x, mine, other,
-    h_recv, s_recv, x_recv, h_send, s_send, x_send,
+    h_recv, s_recv, x_recv, h_send, s_send, x_send, g_send,
 ):
     z, f = lax.axis_index("wa"), lax.axis_index("facet")
     core = f & 1
@@ -456,19 +445,19 @@
     transform(0)
     pl.semaphore_wait(barrier, 7)
 
-    to_h = jnp.where(seat == 0, 2, jnp.where(seat == 2, 3, jnp.where(seat == 3, 1,
-           jnp.where(seat == 6, 4, jnp.where(seat == 4, 5, 7)))))
-    to_s = jnp.where(seat == 1, 6, jnp.where(seat == 3, 4, jnp.where(seat == 4, 3, 1)))
-    sends_h = is_seat(0, 2, 3, 4, 5, 6)
-    takes_h = is_seat(1, 2, 3, 4, 5, 7)
-    sends_x = is_seat(0, 2)
+    to_h = jnp.where(seat == 0, 2, jnp.where(seat == 3, 1, jnp.where(seat == 6, 4, 5)))
+    to_s = jnp.where(seat == 1, 6, jnp.where(seat == 2, 4, jnp.where(seat == 4, 3, 1)))
+    sends_h = is_seat(0, 3, 4, 6)
+    sends_s = is_seat(1, 2, 4, 6)
+    sends_x = is_seat(0, 2, 3, 5)
+    takes_h = is_seat(1, 2, 4, 5, 7)
     away = is_seat(1, 3, 4, 6)
     lag = jnp.where(is_seat(2, 4), 1, 3)
 
-    def copy_h(i, source=mine):
+    def copy_h(i):
         rows = chunk_rows(i)
         return pltpu.make_async_remote_copy(
-            src_ref=source.at[rows], dst_ref=from_h.at[rows], send_sem=h_send.at[i], recv_sem=h_recv.at[i],
+            src_ref=mine.at[rows], dst_ref=from_h.at[rows], send_sem=h_send.at[i], recv_sem=h_recv.at[i],
             device_id=at(to_h), device_id_type=MESH,
         )
 
@@ -476,7 +465,14 @@
         rows = chunk_rows(i)
         return pltpu.make_async_remote_copy(
             src_ref=source.at[rows], dst_ref=from_x.at[rows], send_sem=x_send.at[i], recv_sem=x_recv.at[i],
-            device_id=at(seat | 1), device_id_type=MESH,
+            device_id=at(seat ^ 1), device_id_type=MESH,
+        )
+
+    def copy_g(i):
+        rows = chunk_rows(i)
+        return pltpu.make_async_remote_copy(
+            src_ref=other.at[rows], dst_ref=from_h.at[rows], send_sem=g_send.at[i], recv_sem=h_recv.at[i],
+            device_id=at(7), device_id_type=MESH,
         )
 
     def copy_s(i):
@@ -520,7 +516,7 @@
                     def _():
                         copy_s(i).start()
 
-            @pl.when(seat == 2)
+            @pl.when(is_seat(2, 3, 5))
             def _():
                 for part in range(PARTS):
                     i = t * PARTS + part
@@ -537,8 +533,8 @@
                     i = t * PARTS + part
                     rows = chunk_rows(i)
                     copy_x(i).wait_recv()
-                    keep(other, rows, *plus(rows, image, turn(rows, *halves(from_x, rows))))
-                    copy_h(i, other).start()
+                    keep(mine, rows, *plus(rows, image, turn(rows, *halves(from_x, rows))))
+                    copy_h(i).start()
 
         block = t - lag
 
@@ -555,22 +551,32 @@
                     copy_h(i).wait_recv()
                     keep(mine, rows, *plus(rows, image, turn(rows, *plus(rows, from_h, twice))))
 
-                @pl.when(seat != 1)
+                    copy_s(i).start()
+
+                @pl.when(seat == 2)
                 def _():
                     copy_h(i).wait_recv()
-                    keep(mine, rows, *plus(rows, image, turn(rows, *halves(from_h, rows))))
-
-                @pl.when(is_seat(2, 4, 5))
+                    once = plus(rows, image, turn(rows, *halves(from_h, rows)))
+                    keep(out_ref, rows, *once)
+                    copy_x(i).wait_recv()
+                    keep(mine, rows, *plus(rows, from_x, turn(rows, *once)))
+                    copy_s(i).start()
+
+                @pl.when(seat == 4)
                 def _():
+                    copy_h(i).wait_recv()
+                    once = plus(rows, image, turn(rows, *halves(from_h, rows)))
+                    keep(mine, rows, *once)
+                    copy_s(i).start()
+                    copy_x(i).wait_recv()
+                    keep(other, rows, *plus(rows, from_x, turn(rows, *once)))
+                    copy_g(i).start()
                     copy_h(i).start()
 
-                @pl.when(is_seat(1, 3, 4))
+                @pl.when(is_seat(5, 7))
                 def _():
-                    copy_s(i).start()
-
-                @pl.when(is_seat(2, 5, 7))
-                def _():
-                    out_ref[rows, :] = mine[rows, :]
+                    copy_h(i).wait_recv()
+                    keep(out_ref, rows, *plus(rows, image, turn(rows, *halves(from_h, rows))))
 
         return carry
 
@@ -594,9 +600,13 @@
         def _():
             copy_x(i).wait_send()
 
-        @pl.when(away)
+        @pl.when(sends_s)
         def _():
             copy_s(i).wait_send()
+
+        @pl.when(seat == 4)
+        def _():
+            copy_g(i).wait_send()
 
         return carry
 
@@ -615,12 +625,37 @@
             pltpu.VMEM(band, F32),
         ]
         + [pltpu.VMEM(band, BF16)] * 5
-        + [pltpu.SemaphoreType.DMA((CHUNKS,))] * 6,
+        + [pltpu.SemaphoreType.DMA((CHUNKS,))] * 7,
         compiler_params=pltpu.CompilerParams(
             collective_id=1, has_side_effects=True, vmem_limit_bytes=24 << 20
         ),
         name="chain",
     )(grid, row_table, p_re, p_im)
+
+
+def widen_kernel(band_ref, out_hbm, wide, sems):
+    def copy(i):
+        rows = pl.ds(i * BLOCK, BLOCK)
+        return pltpu.make_async_copy(wide.at[rows], out_hbm.at[rows], sems.at[i])
+
+    for i in range(BLOCKS):
+        rows = pl.ds(i * BLOCK, BLOCK)
+        wide[rows, :] = band_ref[rows, :].astype(F32)
+        copy(i).start()
+    for i in range(BLOCKS):
+        copy(i).wait()
+
+
+def widen(band):
+    return pl.pallas_call(
+        widen_kernel,
+        out_shape=jax.ShapeDtypeStruct(band.shape, F32),
+        in_specs=[VMEM],
+        out_specs=HBM,
+        scratch_shapes=[pltpu.VMEM(band.shape, F32), pltpu.SemaphoreType.DMA((BLOCKS,))],
+        compiler_params=pltpu.CompilerParams(vmem_limit_bytes=8 << 20),
+        name="widen",
+    )(band)
 
 
 def dft_rows():
@@ -636,7 +671,7 @@
     recv, p_re, p_im = route(vis, ang, routes.reshape(1, SUBS), offsets.T, pixel_phase[0])
     grid, row_table = grid_owner(recv.reshape(SUBS * ROWS, 128), jnp.asarray(dft_rows()))
     result = chain(grid, row_table, p_re, p_im)
-    return result.astype(F32).reshape(1, 1, GRID, 2 * GRID)
+    return widen(result).reshape(1, 1, GRID, 2 * GRID)
 
 
 def solution(mesh):

time: 47.6 us -> 46.2 us (0.971); the launches traced: 47 us -> 46.1 us
  other arithmetic: 1.57 us -> 0 us
  Pallas kernels: 45.4 us -> 46.1 us
    reshape x1 -> x0, other arithmetic: 1.57 us -> none  [on_device(): return result.astype(F32).reshape(1, 1, GRID, 2 * GRID)]
    pallas_call x0 -> x1, Pallas kernels: none -> 1.39 us  [widen(): pl.pallas_call(widen_kernel, out_shape=jax.ShapeDtypeStruct(band.shape, F...]
    pallas_call x1, Pallas kernels: 9.22 us -> 8.58 us  [grid_owner(): pl.pallas_call(grid_kernel, out_shape=(band, band), in_specs=[VMEM, HBM],...]
where the time goes in v6:
time: 46.2 us; the launch traced here: 46.1 us
  Pallas kernels  46.1 us (100%)
    pallas_call x1, Pallas kernels, chain(): pl.pallas_call(chain_kernel, out_shape=jax.ShapeDtypeStruct(band, BF16),...  20.1 us
    pallas_call x1, Pallas kernels, route(): pl.pallas_call(route_kernel, out_shape=(jax.ShapeDtypeStruct((SUBS, ROWS,...  16 us
    pallas_call x1, Pallas kernels, grid_owner(): pl.pallas_call(grid_kernel, out_shape=(band, band), in_specs=[VMEM, HBM],...  8.58 us
    pallas_call x1, Pallas kernels, widen(): pl.pallas_call(widen_kernel, out_shape=jax.ShapeDtypeStruct(band.shape, F...  1.39 us

profile of v6, /device:TPU:1, one launch (start us, length us, event | category | flops | bytes accessed | tf_op | source)
XLA Modules:
  0.0 46.1 jit_solution(7380963035120018106)
XLA Ops:
  0.0 16.0 %route.1 = (bf16[128,8,128]{2,1,0:T(8,128)(2,1)S(1)}, f32[512,512]{1,0:T(8,128)S(1)}, f32[512,512]{1,0:T(8,128)S(1)}) custom-call(bf16[128,128]{1,0:T(8,128)(2,1)} %bitcast.14, f32[128,128]{1,0:T(8,128)} %bitcast.13, s32[1,128]{1,0:T(1,128)} %bitcast.16, s32[2,128]{1,0:T(2,128)} %bitcast.15, f32[512,512]{1,0:T(8,128)} %bitcast.12), custom_call_target="tpu_custom_call" | custom-call | tf_op jit(solution)/shard_map/route/pallas_call | solution.py:192
  16.1 8.6 %grid.1 = (bf16[512,1024]{1,0:T(8,128)(2,1)S(1)}, bf16[512,1024]{1,0:T(8,128)(2,1)S(1)}) custom-call(bf16[1024,128]{1,0:T(8,128)(2,1)S(1)} %bitcast.11, bf16[512,1024]{1,0:T(8,128)(2,1)} %constant.2.clone.rows_hbm), custom_call_target="tpu_custom_call" | custom-call | tf_op jit(solution)/shard_map/grid/pallas_call | solution.py:376
  24.6 20.1 %chain.1.band_ref = bf16[512,1024]{1,0:T(8,128)(2,1)S(1)} custom-call(bf16[512,1024]{1,0:T(8,128)(2,1)S(1)} %get-tuple-element.11.grid_ref, bf16[512,1024]{1,0:T(8,128)(2,1)S(1)} %get-tuple-element.12.row_ref, f32[512,512]{1,0:T(8,128)S(1)} %get-tuple-element.13.p_re, f32[512,512]{1,0:T(8,128)S(1)} %get-tuple-element.14.p_im), custom_call_target="tpu_custom_call" | custom-call | tf_op jit(solution)/shard_map/chain/pallas_call | solution.py:618
  44.8 1.4 %widen.1 = f32[512,1024]{1,0:T(8,128)} custom-call(bf16[512,1024]{1,0:T(8,128)(2,1)S(1)} %chain.1.band_ref), custom_call_target="tpu_custom_call" | custom-call | tf_op jit(solution)/shard_map/widen/pallas_call | solution.py:650
